TPU v7x, 256 devices: a whole 4x4x8 slice. The times are simulated.
256 devices in a mesh: dp: 16 (over z, core), fsdp: 16 (over y, x).
Axes of the slice: x: 4, y: 4, z: 8, core: 2. Of those that a mesh axis runs over, the one named last changes fastest.
Arguments:
- features: bfloat16 [16, 16, 32, 32, 512], P('fsdp', None, 'dp'), may hold values from -6 to 6
- conv_weight: bfloat16 [3, 3, 512, 8], replicated, may hold values from -0.046875 to 0.046875
- vae_noise: float32 [16, 16, 4096], P('dp', 'fsdp'), may hold values from -6 to 6
- flips: int32 [16, 16, 4], P('dp', 'fsdp'), may hold values from 0 to 1
- crops: int32 [16, 16, 4, 2], P('dp', 'fsdp'), may hold values from 0 to 4
- tsteps: int32 [16, 16, 4], P('dp', 'fsdp'), may hold values from 0 to 999
- diffusion_noise: float32 [16, 16, 4, 4096], P('dp', 'fsdp'), may hold values from -6 to 6
- selected: int32 [16, 16], P('dp', 'fsdp'), may hold values from 0 to 1, as said below
- w_patch: bfloat16 [16, 384], replicated, may hold values from -1.5 to 1.5
- w_time: bfloat16 [256, 384], replicated, may hold values from -0.375 to 0.375
- w_ada: bfloat16 [384, 1152], replicated, may hold values from -0.3125 to 0.3125
- w_fc1: bfloat16 [384, 1536], P(None, 'fsdp'), may hold values from -1 to 1
- w_fc2: bfloat16 [384, 1536], P(None, 'fsdp'), may hold values from -1 to 1
- w_final: bfloat16 [384, 16], replicated, may hold values from -0.3125 to 0.3125
- noise_fc1: float32 [384, 1536], P(None, 'fsdp'), may hold values from -6 to 6
- noise_fc2: float32 [384, 1536], P(None, 'fsdp'), may hold values from -6 to 6
Outputs:
- update_fc1: float32 [384, 1536], P(None, 'fsdp')
- update_fc2: float32 [384, 1536], P(None, 'fsdp')
- mean_loss: float32 [], replicated
- latent_moments: float32 [16, 16, 8192], P('dp', 'fsdp')
Inputs may be any that keep to these rules, and one draw needn't show every extreme that they name: `selected`: exactly 128 slots are 1.
All inputs are finite; a program needn't handle non-finite values.
Results may differ from a plain program's by a relative error of at most 0.00091.
Values may be sent and summed in bfloat16 or wider, within the bound.
A program may use at most 64 MiB of HBM per device.

v0:
```python
from functools import partial
import functools
import math

import jax
import jax.numpy as jnp
from jax import lax
from jax.sharding import Mesh
from jax.sharding import PartitionSpec as P

TSTEPS = 1000
DP = ("dp_0", "dp_1")
FSDP = ("fsdp_0", "fsdp_1")
DP_FSDP = ("dp_0", "dp_1", "fsdp_0", "fsdp_1")


clip_offset = 1e-05
noise_weight = 16.0
norm_epsilon = 1e-06


def with_halo(value, sides, width):
    for axis, dim in sides:
        size, length = (lax.axis_size(axis), value.shape[dim])
        up = [(i, (i + 1) % size) for i in range(size - 1)]
        down = [(j, i) for i, j in up]
        last = lax.slice_in_dim(value, length - width, length, axis=dim)
        first = lax.slice_in_dim(value, 0, width, axis=dim)
        before = lax.ppermute(last, axis, up)
        after = lax.ppermute(first, axis, down)
        value = jnp.concatenate([before, value, after], axis=dim)
    return value


def turned_gather(arrays, axis, dims):
    turned = [jnp.moveaxis(a, dim, 0) for a, dim in zip(arrays, dims)]
    widths = [t[0].size for t in turned]
    both = jnp.concatenate([t.reshape(-1, w) for t, w in zip(turned, widths)], axis=1)
    whole = lax.all_gather(both, axis, axis=0, tiled=True)
    tiles = jnp.split(whole, [sum(widths[:k]) for k in range(1, len(widths))], axis=1)
    return tuple(
        (
            jnp.moveaxis(b.reshape(-1, *t.shape[1:]), 0, dim)
            for b, t, dim in zip(tiles, turned, dims)
        )
    )


def in_blocks(value, dim, length):
    before, after = (value.shape[:dim], value.shape[dim + 1 :])
    return jnp.moveaxis(value.reshape(*before, length, -1, *after), dim, 0)


def one_scatter(arrays, axis, dims):
    length = lax.axis_size(axis)
    tiles = [in_blocks(a, dim, length) for a, dim in zip(arrays, dims)]
    lines = jnp.concatenate([b.reshape(length, -1) for b in tiles], axis=1)
    width = max(16, -(-lines.shape[1] // 1024) * 8)
    lines = jnp.pad(lines, ((0, 0), (0, width * 128 - lines.shape[1]))).reshape(-1, 128)
    ravelled, at, gathered = (lax.psum_scatter(lines, axis, tiled=True).reshape(-1), 0, [])
    for b in tiles:
        part = b[0]
        gathered.append(ravelled[at : at + part.size].reshape(part.shape))
        at += part.size
    return tuple(gathered)


def together(arrays, axis):
    ends = [0]
    for a in arrays:
        ends.append(ends[-1] + a.size)
    total = lax.psum(jnp.concatenate([a.ravel() for a in arrays]), axis)
    return tuple((total[b:e].reshape(a.shape) for a, b, e in zip(arrays, ends, ends[1:])))


def over_axes(value, axes):
    return functools.reduce(lax.psum, axes, value)


def layer_norm(values):
    center = values - jnp.mean(values, axis=-1, keepdims=True)
    variance = jnp.mean(center * center, axis=-1, keepdims=True)
    return center * lax.rsqrt(variance + norm_epsilon)


def position_table(side_cells, width):
    quarter = width // 4
    frequency = 1.0 / 10000.0 ** (jnp.arange(quarter, dtype=jnp.float32) / quarter)
    positions = jnp.arange(side_cells, dtype=jnp.float32)
    angles = positions[:, None] * frequency[None, :]
    line_table = jnp.concatenate([jnp.sin(angles), jnp.cos(angles)], axis=1)
    row_part = jnp.repeat(line_table, side_cells, axis=0)
    col_part = jnp.tile(line_table, (side_cells, 1))
    return jnp.concatenate([row_part, col_part], axis=1)


def time_features(steps_in, width):
    half_width = width // 2
    rates = jnp.exp(-math.log(10000.0) * jnp.arange(half_width, dtype=jnp.float32) / half_width)
    phases = steps_in.astype(jnp.float32)[:, None] * rates[None, :]
    return jnp.concatenate([jnp.cos(phases), jnp.sin(phases)], axis=1)


def alpha_bars(steps_in, horizon):
    beta_table = jnp.linspace(0.0001, 0.02, horizon, dtype=jnp.float32)
    alpha_bar = jnp.cumprod(1.0 - beta_table)
    matches = jnp.arange(horizon, dtype=jnp.int32)[None, :] == steps_in[:, None]
    return jnp.sum(jnp.where(matches, alpha_bar[None, :], 0.0), axis=1)


def augment(latent, mirror, crop_at):
    side_cells = latent.shape[0]
    mirrored = jnp.where(mirror == 1, latent[:, ::-1, :], latent)
    padded = jnp.pad(mirrored, ((2, 2), (2, 2), (0, 0)))
    starts = (crop_at[0], crop_at[1], jnp.int32(0))
    return lax.dynamic_slice(padded, starts, (side_cells, side_cells, latent.shape[2]))


def patchify(grid):
    views_count = grid.shape[0]
    half_side = grid.shape[1] // 2
    channels = grid.shape[3]
    blocks = grid.reshape(views_count, half_side, 2, half_side, 2, channels)
    blocks = blocks.transpose(0, 1, 3, 2, 4, 5)
    return blocks.reshape(views_count * half_side * half_side, 4 * channels)


def row_tap_sums(local_rows, kernel):
    image_count, row_count, side_cells, channels = local_rows.shape
    out_width = kernel.shape[3]
    tap_matrix = kernel.transpose(2, 0, 1, 3).reshape(channels, 9 * out_width)
    tap_values = jnp.dot(
        local_rows.reshape(-1, channels), tap_matrix, preferred_element_type=jnp.float32
    )
    tap_values = tap_values.reshape(image_count, row_count, side_cells, 3, 3, out_width)
    tap_values = jnp.pad(tap_values, ((0, 0), (0, 0), (1, 1), (0, 0), (0, 0), (0, 0)))
    summed = jnp.zeros((image_count, row_count, side_cells, 3, out_width), jnp.float32)
    for col_tap in range(3):
        summed = summed + tap_values[:, :, col_tap : col_tap + side_cells, :, col_tap, :]
    return summed


def example_terms(mean_part, logvar, vae_eps, mirror, crop_at, steps_in, noise, weights):
    w_patch, w_time, w_ada, w_fc1, w_fc2, w_final = weights
    side_cells = mean_part.shape[0]
    channels = mean_part.shape[2]
    views_count = mirror.shape[0]
    width = w_fc1.shape[0]
    latent = mean_part + jnp.exp(0.5 * logvar) * vae_eps.reshape(mean_part.shape)
    augmented = jax.vmap(augment, in_axes=(None, 0, 0))(latent, mirror, crop_at)
    alpha_bar = alpha_bars(steps_in, TSTEPS)
    noise_grid = noise.reshape(views_count, side_cells, side_cells, channels)
    keep_part = jnp.sqrt(alpha_bar)[:, None, None, None]
    blend_part = jnp.sqrt(1.0 - alpha_bar)[:, None, None, None]
    noised = keep_part * augmented + blend_part * noise_grid
    patches = patchify(noised).astype(jnp.bfloat16)
    target = patchify(noise_grid)
    half_side = side_cells // 2
    per_view = half_side * half_side
    tokens = jnp.dot(patches, w_patch, preferred_element_type=jnp.float32)
    tokens = tokens + jnp.tile(position_table(half_side, width), (views_count, 1))
    stamp = time_features(steps_in, w_time.shape[0]).astype(jnp.bfloat16)
    conditioning = jax.nn.silu(jnp.dot(stamp, w_time, preferred_element_type=jnp.float32))
    modulation = jnp.dot(
        conditioning.astype(jnp.bfloat16), w_ada, preferred_element_type=jnp.float32
    )
    offset_rows = jnp.repeat(modulation[:, :width], per_view, axis=0)
    scale_rows = jnp.repeat(modulation[:, width : 2 * width], per_view, axis=0)
    gate_rows = jnp.repeat(modulation[:, 2 * width :], per_view, axis=0)
    modulated = (layer_norm(tokens) * (1.0 + scale_rows) + offset_rows).astype(jnp.bfloat16)
    preact = jnp.dot(modulated, w_fc1, preferred_element_type=jnp.float32)
    hidden, gelu_back = jax.vjp(partial(jax.nn.gelu, approximate=True), preact)
    hidden_low = hidden.astype(jnp.bfloat16)
    branch = lax.dot_general(
        hidden_low, w_fc2, (((1,), (1,)), ((), ())), preferred_element_type=jnp.float32
    )
    mixed_rows = tokens + gate_rows * branch
    final_norm, norm_back = jax.vjp(layer_norm, mixed_rows)
    final_low = final_norm.astype(jnp.bfloat16)
    predicted = jnp.dot(final_low, w_final, preferred_element_type=jnp.float32)
    residue = predicted - target
    entries = residue.shape[0] * residue.shape[1]
    loss_value = jnp.sum(residue * residue) / entries
    grad_pred = (residue * (2.0 / entries)).astype(jnp.bfloat16)
    grad_final = lax.dot_general(
        grad_pred, w_final, (((1,), (1,)), ((), ())), preferred_element_type=jnp.float32
    )
    grad_mixed = norm_back(grad_final)[0]
    grad_branch = (gate_rows * grad_mixed).astype(jnp.bfloat16)
    grad_fc2 = lax.dot_general(
        grad_branch, hidden_low, (((0,), (0,)), ((), ())), preferred_element_type=jnp.float32
    )
    grad_hidden = jnp.dot(grad_branch, w_fc2, preferred_element_type=jnp.float32)
    grad_pre = gelu_back(grad_hidden)[0].astype(jnp.bfloat16)
    grad_fc1 = lax.dot_general(
        modulated, grad_pre, (((0,), (0,)), ((), ())), preferred_element_type=jnp.float32
    )
    return (loss_value, grad_fc1, grad_fc2)


def clip_pair(grad_fc1, grad_fc2):
    squares = jnp.sum(grad_fc1 * grad_fc1) + jnp.sum(grad_fc2 * grad_fc2)
    root_mean = jnp.sqrt(squares / (grad_fc1.size + grad_fc2.size))
    factor = 1.0 / (root_mean + clip_offset)
    return (grad_fc1 * factor, grad_fc2 * factor)


def selected_terms(chosen, mean_part, logvar, vae_eps, mirror, crop_at, steps_in, noise, weights):

    def compute():
        loss_value, grad_fc1, grad_fc2 = example_terms(
            mean_part, logvar, vae_eps, mirror, crop_at, steps_in, noise, weights
        )
        clipped_fc1, clipped_fc2 = clip_pair(grad_fc1, grad_fc2)
        return (loss_value, clipped_fc1, clipped_fc2)

    def skipped():
        zeros = jnp.zeros((weights[3].shape[0], weights[3].shape[1]), jnp.float32)
        return (jnp.zeros((), jnp.float32), zeros, zeros)

    return lax.cond(chosen == 1, compute, skipped)


def per_device(
    features,
    conv_weight,
    vae_noise,
    flips,
    crops,
    tsteps,
    diffusion_noise,
    selected,
    w_patch,
    w_time,
    w_ada,
    w_fc1,
    w_fc2,
    w_final,
    noise_fc1,
    noise_fc2,
):
    local_rows = features[0]
    slot_count = local_rows.shape[0]
    row_count = local_rows.shape[1]
    side_cells = local_rows.shape[2]
    out_width = conv_weight.shape[3]
    channels = out_width // 2
    row_parts = row_tap_sums(local_rows, conv_weight)
    rim_terms = jnp.concatenate([row_parts[:, :, :, 0, :], row_parts[:, :, :, 2, :]], axis=3)
    rim_terms = rim_terms.reshape(slot_count, row_count, side_cells * 2 * out_width)
    rimmed = with_halo(rim_terms, ((DP, 1),), 1)
    rimmed = rimmed.reshape(slot_count, row_count + 2, side_cells, 2 * out_width)
    slab_moments = (
        row_parts[:, :, :, 1, :]
        + rimmed[:, 0:row_count, :, :out_width]
        + rimmed[:, 2 : row_count + 2, :, out_width:]
    )
    flattened = slab_moments.reshape(slot_count, row_count, side_cells * out_width)
    moments = lax.all_to_all(flattened, DP, split_axis=0, concat_axis=1, tiled=True).reshape(
        -1, side_cells, side_cells, out_width
    )
    latent_moments = moments.reshape(moments.shape[0], 1, side_cells * side_cells * out_width)
    full_fc1, full_fc2 = turned_gather((w_fc1, w_fc2), FSDP, (1, 1))
    weights = (w_patch, w_time, w_ada, full_fc1, full_fc2, w_final)
    loss_local = jnp.zeros((), jnp.float32)
    summed_fc1 = jnp.zeros(full_fc1.shape, jnp.float32)
    summed_fc2 = jnp.zeros(full_fc2.shape, jnp.float32)
    moment = moments[0]
    loss_value, clipped_fc1, clipped_fc2 = selected_terms(
        selected[0, 0],
        moment[..., :channels],
        moment[..., channels:],
        vae_noise[0, 0],
        flips[0, 0],
        crops[0, 0],
        tsteps[0, 0],
        diffusion_noise[0, 0],
        weights,
    )
    loss_local = loss_local + loss_value
    summed_fc1 = summed_fc1 + clipped_fc1
    summed_fc2 = summed_fc2 + clipped_fc2
    selected_count = selected.shape[0] * lax.axis_size(DP) * lax.axis_size(FSDP) // 2
    owned_fc1, owned_fc2 = one_scatter((summed_fc1, summed_fc2), FSDP, (1, 1))
    shard_fc1, shard_fc2 = together((owned_fc1, owned_fc2), DP)
    loss_all = over_axes(loss_local, DP_FSDP)
    update_fc1 = (shard_fc1 + noise_weight * noise_fc1) / selected_count
    update_fc2 = (shard_fc2 + noise_weight * noise_fc2) / selected_count
    return (update_fc1, update_fc2, loss_all / selected_count, latent_moments)


def solution(mesh):
    split = Mesh(mesh.devices.reshape(8, 2, 4, 4), ("dp_0", "dp_1", "fsdp_0", "fsdp_1"))
    return jax.shard_map(
        per_device,
        mesh=split,
        in_specs=(
            P(FSDP, None, DP, None, None),
            P(),
            P(DP, FSDP, None),
            P(DP, FSDP, None),
            P(DP, FSDP, None, None),
            P(DP, FSDP, None),
            P(DP, FSDP, None, None),
            P(DP, FSDP),
            P(),
            P(),
            P(),
            P(None, FSDP),
            P(None, FSDP),
            P(),
            P(None, FSDP),
            P(None, FSDP),
        ),
        out_specs=(P(None, FSDP), P(None, FSDP), P(), P(DP, FSDP, None)),
        check_vma=False,
    )
```

profile of v0, /device:TPU:1, one launch (start us, length us, event | category | flops | bytes accessed | tf_op | source)
XLA Modules:
  0.0 370.9 jit_solution(3611342339859881097)
XLA Ops:
  11.6 5.2 %collective-permute-start.1 = (f32[16,1,512]{2,0,1:T(8,128)S(1)}, f32[16,1,512]{2,0,1:T(8,128)S(1)}, u32[]{:S(2)}, u32[]{:S(2)}) collective-permute-start(f32[16,1,512]{2,0,1:T(8,128)S(1)} %get-tuple-element.235), channel_id=1, source_target_pairs={{16,0},{32,16},{48,32},{64,48},{80,64},{96,80},{112,96},{128,112},... | collective-permute-start | bytes 98312 | tf_op jit(solution)/shard_map/ppermute | solution.py:30
  21.1 10.1 %all-to-all-start = ((f32[16,2,256]{2,1,0:T(2,128)}), f32[16,2,256]{2,1,0:T(2,128)S(1)}, u32[]{:S(2)}, u32[]{:S(2)}) async-start(f32[16,2,256]{2,1,0:T(2,128)} %copy.140), calls=%async_computation | async-start | bytes 65536 | tf_op jit(solution)/shard_map/all_to_all | solution.py:259
  31.3 33.4 %all-gather.2.cloned.1.call-done = bf16[1536,768]{1,0:T(8,128)(2,1)} async-done(((bf16[96,768]{1,0:T(8,128)(2,1)}), bf16[1536,768]{1,0:T(8,128)(2,1)}) %all-gather.2.cloned.1.call-update) | async-done | bytes 2359312 | tf_op jit(solution)/shard_map/all_gather | solution.py:39
  64.6 3.4 slice_bitcast_fusion
  68.1 75.5 %conditional.1 = (f32[]{:T(128)}, f32[384,1536]{1,0:T(8,128)}, f32[384,1536]{1,0:T(8,128)}) conditional(s32[]{:T(128)} %bitcast.11, () %tuple.19, (s32[1,1,4]{2,1,0:T(1,128)S(1)}, s32[1,1,4]{2,1,0:T(1,128)S(1)}, f32[16,2,256]{2,1,0:T(2,128)S(1)}, f32[1,1,4096]{2,1,0:T(1,128)S(1)}, s32[1,1,4,2]{2,3,1,0:T(2,128)S(1)}, ...), branch_computations={%region_0.1_spmd, %region_1.14_spmd} | conditional | flops 6159788032 | bytes 192987072 | solution.py:221
  68.1 3.2 reshape_squeeze.8
  71.2 2.4 copy.133
  82.9 10.5 %while.1 = (s32[]{:T(128)}, f32[4,36,36,4]{2,3,1,0:T(4,128)S(1)}, s32[4,4]{1,0:T(4,128)S(1)}, f32[4,32,32,4]{2,3,1,0:T(4,128)S(1)}, s32[]{:T(128)}) while((s32[]{:T(128)}, f32[4,36,36,4]{2,3,1,0:T(4,128)S(1)}, s32[4,4]{1,0:T(4,128)S(1)}, f32[4,32,32,4]{2,3,1,0:T(4,128)S(1)}, s32[]{:T(128)}) %tuple.68), condition=%wide.while_cond, body=%wide.while_body.sunk | while | flops 2 | bytes 131217 | solution.py:116
  83.6 2.0 dynamic-slice_dynamic-update-slice_fusion.2
  86.2 2.0 dynamic-slice_dynamic-update-slice_fusion.2
  88.8 2.0 dynamic-slice_dynamic-update-slice_fusion.2
  93.5 2.2 copy.127
  95.6 3.7 fusion.8
  99.3 2.3 copy.128
  114.1 4.0 %fusion.61 = (f32[1024]{0:T(1024)S(1)}, f32[1024,384]{0,1:T(8,128)S(1)}) fusion(f32[1024,384]{0,1:T(8,128)S(1)} %copy-done.3, f32[1024,384]{0,1:T(8,128)S(1)} %bitcast.133, bf16[384,1536]{0,1:T(8,128)(2,1)S(1)} %copy-done.10, f32[1024,1536]{1,0:T(8,128)S(1)} %fusion.64), kind=kOutput, calls=%fused_computation.125 | convolution fusion | flops 1223293952 | bytes 12193792 | tf_op jit(solution)/shard_map/cond/branch_1_fun/dot_general | solution.py:174
  123.2 3.5 multiply_reduce_fusion
  126.7 11.1 %multiply_reduce_fusion.1 = (f32[]{:T(128)}, f32[384,1536]{1,0:T(8,128)}) fusion(bf16[1024,384]{0,1:T(8,128)(2,1)S(1)} %add_convert_fusion.1, f32[1024,1536]{1,0:T(8,128)} %copy-done.4, bf16[1024,384]{0,1:T(8,128)(2,1)} %copy-done.12, bf16[384,1536]{0,1:T(8,128)(2,1)} %get-tuple-element.184), kind=kOutput, calls=%fused_computation.14 | convolution fusion | flops 2448556032 | bytes 11403268 | tf_op jit(solution)/shard_map/cond/branch_1_fun/dot_general | solution.py:195
  139.2 4.3 %broadcast_multiply_fusion = (f32[384,1536]{1,0:T(8,128)}, f32[384,1536]{1,0:T(8,128)}) fusion(f32[384,1536]{1,0:T(8,128)S(1)} %get-tuple-element.223, f32[]{:T(128)S(6)} %div.64, f32[384,1536]{1,0:T(8,128)} %get-tuple-element.221), kind=kLoop, calls=%fused_computation.25 | loop fusion | flops 1179648 | bytes 9437188 | tf_op jit(solution)/shard_map/cond/branch_1_fun/mul | solution.py:205
  143.5 2.0 copy.145
  145.6 2.3 copy.146
  147.9 4.2 %reshape.200 = f32[16,36864]{1,0:T(8,128)} reshape(f32[16,384,96]{2,1,0:T(8,128)} %copy.146) | data formatting | bytes 4718592 | tf_op jit(solution)/shard_map/reshape | solution.py:57
  152.1 2.0 copy.143
  154.2 2.3 copy.144
  156.5 4.4 %reshape.198 = f32[16,36864]{1,0:T(8,128)} reshape(f32[16,384,96]{2,1,0:T(8,128)} %copy.144) | data formatting | bytes 4718592 | tf_op jit(solution)/shard_map/reshape | solution.py:57
  160.9 4.1 %pad_maximum_fusion.2 = f32[16,73728]{1,0:T(8,128)} fusion(f32[16,36864]{1,0:T(8,128)S(1)} %copy-done.5, f32[16,36864]{1,0:T(8,128)} %reshape.198), kind=kLoop, calls=%fused_computation.95 | loop fusion | flops 1179648 | bytes 9437184 | tf_op jit(solution)/shard_map/concatenate | solution.py:57
  164.9 4.2 %reshape.201 = f32[9216,128]{1,0:T(8,128)} reshape(f32[16,73728]{1,0:T(8,128)} %pad_maximum_fusion.2) | data formatting | bytes 9437184 | tf_op jit(solution)/shard_map/reshape | solution.py:59
  169.2 82.4 %reduce-scatter.2.cloned.1.call-done = f32[576,128]{1,0:T(8,128)} async-done(((f32[9216,128]{1,0:T(8,128)}), f32[576,128]{1,0:T(8,128)}) %reduce-scatter.2.cloned.1.call-update) | async-done | bytes 294928 | tf_op jit(solution)/shard_map/reduce_scatter | solution.py:60
  253.4 14.8 %psum.36 = f32[]{:T(128)} all-reduce(f32[]{:T(128)} %get-tuple-element.79), channel_id=1, replica_groups=mesh['dp_0'=8,'dp_1'=2,'fsdp_0'=4,'fsdp_1'=4] {'dp_0'}, use_global_device_ids=true, to_apply=%region_16.17 | all-reduce | flops 1 | bytes 8 | tf_op jit(solution)/shard_map/psum | solution.py:77
  268.3 8.8 %psum.37 = f32[]{:T(128)} all-reduce(f32[]{:T(128)} %psum.36), channel_id=1, replica_groups=mesh['dp_0'=8,'dp_1'=2,'fsdp_0'=4,'fsdp_1'=4] {'dp_1'}, use_global_device_ids=true, to_apply=%region_17.18 | all-reduce | flops 1 | bytes 8 | tf_op jit(solution)/shard_map/psum | solution.py:77
  277.3 9.3 %psum.38 = f32[]{:T(128)} all-reduce(f32[]{:T(128)} %psum.37), channel_id=1, replica_groups=mesh['dp_0'=8,'dp_1'=2,'fsdp_0'=4,'fsdp_1'=4] {'fsdp_0'}, use_global_device_ids=true, to_apply=%region_18.19 | all-reduce | flops 1 | bytes 8 | tf_op jit(solution)/shard_map/psum | solution.py:77
  287.3 6.7 %psum.39 = f32[]{:T(128)} all-reduce(f32[]{:T(128)} %psum.38), channel_id=1, replica_groups=mesh['dp_0'=8,'dp_1'=2,'fsdp_0'=4,'fsdp_1'=4] {'fsdp_1'}, use_global_device_ids=true, to_apply=%region_19.20 | all-reduce | flops 1 | bytes 8 | tf_op jit(solution)/shard_map/psum | solution.py:77
  294.6 65.8 %all-reduce.5.cloned.1.call-done = f32[73728]{0:T(1024)} async-done(((f32[73728]{0:T(1024)}), f32[73728]{0:T(1024)}) %all-reduce.5.cloned.1.call-update) | async-done | bytes 294928 | tf_op jit(solution)/shard_map/psum | solution.py:72
  (168 shorter events, 43.9 us)
Async XLA Ops:
  7.2 1.8 copy-start
  7.2 57.5 %all-gather.2.cloned.1.call-start = ((), (), s32[]{:S(2)}) async-start(), calls=%async_computation.2 | async-start | bytes 2506752 | tf_op jit(solution)/shard_map/all_gather | solution.py:39
  11.6 7.7 %collective-permute-start.1 = (f32[16,1,512]{2,0,1:T(8,128)S(1)}, f32[16,1,512]{2,0,1:T(8,128)S(1)}, u32[]{:S(2)}, u32[]{:S(2)}) collective-permute-start(f32[16,1,512]{2,0,1:T(8,128)S(1)} %get-tuple-element.235), channel_id=1, source_target_pairs={{16,0},{32,16},{48,32},{64,48},{80,64},{96,80},{112,96},{128,112},... | collective-permute-start | bytes 98312 | tf_op jit(solution)/shard_map/ppermute | solution.py:30
  16.8 3.1 collective-permute-start
  21.1 46.9 %all-to-all-start = ((f32[16,2,256]{2,1,0:T(2,128)}), f32[16,2,256]{2,1,0:T(2,128)S(1)}, u32[]{:S(2)}, u32[]{:S(2)}) async-start(f32[16,2,256]{2,1,0:T(2,128)} %copy.140), calls=%async_computation | async-start | bytes 65536 | tf_op jit(solution)/shard_map/all_to_all | solution.py:259
  31.2 36.8 %copy-start.17 = (f32[1,1,4,4096]{3,2,1,0:T(4,128)S(1)}, f32[1,1,4,4096]{3,2,1,0:T(4,128)}, u32[]{:S(2)}) copy-start(f32[1,1,4,4096]{3,2,1,0:T(4,128)} %param.24) | copy-start | bytes 196612
  31.2 36.8 %copy-start.18 = (bf16[384,16]{0,1:T(8,128)(2,1)S(1)}, bf16[384,16]{0,1:T(8,128)(2,1)}, u32[]{:S(2)}) copy-start(bf16[384,16]{0,1:T(8,128)(2,1)} %param.31) | copy-start | bytes 36868
  31.2 36.8 %copy-start.19 = (f32[1,1,4096]{2,1,0:T(1,128)S(1)}, f32[1,1,4096]{2,1,0:T(1,128)}, u32[]{:S(2)}) copy-start(f32[1,1,4096]{2,1,0:T(1,128)} %param.20) | copy-start | bytes 49156
  31.2 36.8 %copy-start.20 = (s32[1,1,4,2]{2,3,1,0:T(2,128)S(1)}, s32[1,1,4,2]{2,3,1,0:T(2,128)}, u32[]{:S(2)}) copy-start(s32[1,1,4,2]{2,3,1,0:T(2,128)} %param.22) | copy-start | bytes 100
  31.2 36.8 %copy-start.21 = (s32[1,1,4]{2,1,0:T(1,128)S(1)}, s32[1,1,4]{2,1,0:T(1,128)}, u32[]{:S(2)}) copy-start(s32[1,1,4]{2,1,0:T(1,128)} %param.23) | copy-start | bytes 52
  31.2 36.8 %copy-start.24 = (s32[1,1,4]{2,1,0:T(1,128)S(1)}, s32[1,1,4]{2,1,0:T(1,128)}, u32[]{:S(2)}) copy-start(s32[1,1,4]{2,1,0:T(1,128)} %param.21) | copy-start | bytes 52
  31.2 220.4 %reduce-scatter.2.cloned.1.call-start = ((), (), s32[]{:S(2)}) async-start(), calls=%async_computation.3 | async-start | bytes 5013504 | tf_op jit(solution)/shard_map/reduce_scatter | solution.py:60
  68.1 9.5 %copy-start.22 = (s32[1,1,4]{2,1,0:T(1,128)}, s32[1,1,4]{2,1,0:T(1,128)S(1)}, u32[]{:S(2)}) copy-start(s32[1,1,4]{2,1,0:T(1,128)S(1)} %get-tuple-element.89) | copy-start | bytes 52 | tf_op jit(solution)/shard_map/cond
  99.3 4.6 %copy-start.23 = (s32[1,1,4]{2,1,0:T(1,128)S(1)}, s32[1,1,4]{2,1,0:T(1,128)}, u32[]{:S(2)}) copy-start(s32[1,1,4]{2,1,0:T(1,128)} %copy-done.22) | copy-start | bytes 52 | tf_op jit(solution)/shard_map/cond
  99.3 4.7 %copy-start.11 = (bf16[384,1152]{1,0:T(8,128)(2,1)S(1)}, bf16[384,1152]{1,0:T(8,128)(2,1)}, u32[]{:S(2)}) copy-start(bf16[384,1152]{1,0:T(8,128)(2,1)} %get-tuple-element.96) | copy-start | bytes 2654212 | tf_op jit(solution)/shard_map/cond
  101.6 2.3 copy-start.14
  103.8 6.0 %copy-start.2 = (f32[1024,384]{0,1:T(8,128)}, f32[1024,384]{0,1:T(8,128)S(1)}, u32[]{:S(2)}) copy-start(f32[1024,384]{0,1:T(8,128)S(1)} %get-tuple-element.213) | copy-start | bytes 4718596 | tf_op jit(solution)/shard_map/cond
  109.2 1.4 copy-start.8
  111.9 1.9 copy-start.3
  111.9 1.9 copy-start.6
  111.9 2.2 copy-start.10
  114.1 4.0 %copy-start.4 = (f32[1024,1536]{1,0:T(8,128)}, f32[1024,1536]{1,0:T(8,128)S(1)}, u32[]{:S(2)}) copy-start(f32[1024,1536]{1,0:T(8,128)S(1)} %fusion.64) | copy-start | bytes 18874372 | tf_op jit(solution)/shard_map/cond
  114.1 4.2 %copy-start.13 = (f32[1024,16]{0,1:T(8,128)S(1)}, f32[1024,16]{0,1:T(8,128)}, u32[]{:S(2)}) copy-start(f32[1024,16]{0,1:T(8,128)} %reshape.185) | copy-start | bytes 196612 | tf_op jit(solution)/shard_map/cond
  119.9 2.7 slice-start
  120.3 1.6 copy-start.7
  120.3 2.9 slice-start.1
  123.2 3.5 copy-start.12
  156.5 4.4 %copy-start.5 = (f32[16,36864]{1,0:T(8,128)S(1)}, f32[16,36864]{1,0:T(8,128)}, u32[]{:S(2)}) copy-start(f32[16,36864]{1,0:T(8,128)} %reshape.200) | copy-start | bytes 7077892
  169.1 99.1 %copy-start.15 = (f32[384,96]{0,1:T(8,128)S(1)}, f32[384,96]{0,1:T(8,128)}, u32[]{:S(2)}) copy-start(f32[384,96]{0,1:T(8,128)} %param.32) | copy-start | bytes 442372
  169.1 108.0 %copy-start.16 = (f32[384,96]{0,1:T(8,128)S(1)}, f32[384,96]{0,1:T(8,128)}, u32[]{:S(2)}) copy-start(f32[384,96]{0,1:T(8,128)} %param.33) | copy-start | bytes 442372
  169.2 191.3 %all-reduce.5.cloned.1.call-start = ((), (), s32[]{:S(2)}) async-start(), calls=%async_computation.4 | async-start | bytes 589824 | tf_op jit(solution)/shard_map/psum | solution.py:72
  252.6 110.7 %copy-start.1 = (bf16[1,16,2,32,512]{4,3,2,1,0:T(8,128)(2,1)S(1)}, bf16[1,16,2,32,512]{4,3,2,1,0:T(8,128)(2,1)}, u32[]{:S(2)}) copy-start(bf16[1,16,2,32,512]{4,3,2,1,0:T(8,128)(2,1)} %param.18) | copy-start | bytes 3145732
  (1 other events, 1.3 us)
Sparse Core Ops, SparseCore 0:
  11.0 53.5 all-gather.1
  169.3 82.2 reduce-scatter.1
  254.0 106.4 all-reduce.4
where the time goes:
time: 372 us; the launch traced here: 371 us
  waiting for transfers between devices  182 us (49%)
  local copies, waits for them, and re-layouts  67.3 us (18%)
  blocking collectives  39.6 us (11%)
  matrix products  25.8 us (7%)
  other arithmetic  20 us (5%)
  starting transfers between devices  17.3 us (5%)
  between operations  16.4 us (4%)
    reduce_scatter x1, waiting for transfers between devices, one_scatter(): lax.psum_scatter(lines, axis, tiled=True).reshape(-1)  82.4 us
    psum x1, waiting for transfers between devices, together(): total = lax.psum(jnp.concatenate([a.ravel() for a in arrays]), axis)  65.8 us
    psum x4, blocking collectives, over_axes(): return functools.reduce(lax.psum, axes, value)  39.6 us
    all_gather x1, waiting for transfers between devices, turned_gather(): whole = lax.all_gather(both, axis, axis=0, tiled=True)  33.4 us
    dot_general x1, matrix products, example_terms(): lax.dot_general(modulated, grad_pre, (((0,), (0,)), ((), ())), preferred_...  11.1 us
    gather x12, local copies, waits for them, and re-layouts  10.4 us
    all_to_all x1, starting transfers between devices, per_device(): lax.all_to_all(flattened, DP, split_axis=0, concat_axis=1, tiled=True)  10.1 us
    cond x38, local copies, waits for them, and re-layouts  8.65 us
  transfers between devices with their start and end apart: 6, of which 4 were waited for; matrix products, arithmetic and copies ran while one was open for 2% of the time, Pallas kernels for 0%

commit v1 on v0

v1 whole, which is shorter than its diff:
```python
import math

import jax
import jax.numpy as jnp
import ml_dtypes
import numpy as np
from jax import lax
from jax.experimental import pallas as pl
from jax.experimental.pallas import tpu as pltpu
from jax.sharding import Mesh
from jax.sharding import PartitionSpec as P

MESH = pl.DeviceIdType.MESH
DP = ("dp_0", "dp_1")
FSDP = ("fsdp_0", "fsdp_1")
NZ, NC, NY, NX = 8, 2, 4, 4
NDP = NZ * NC
D, FF, TOK, FCH = 384, 1536, 1024, 512
SHARD = FF // (NY * NX)
HALF = SHARD // 2
SIDE, LC, AUG, TSTEPS = 32, 4, 4, 1000
SELECTED = 128
CHUNK = 384
PIECE = 5
TILES = NZ * PIECE
USED_TILES = (SHARD // 8) * (D // 128)
clip_offset = 1e-05
noise_weight = 16.0
norm_epsilon = 1e-06
VMEM_SPEC = pl.BlockSpec(memory_space=pltpu.VMEM)
SMEM_SPEC = pl.BlockSpec(memory_space=pltpu.SMEM)
F32, BF16 = jnp.float32, jnp.bfloat16


def three_parts(table):
    high = table.astype(np.float32).astype(ml_dtypes.bfloat16)
    rest = table.astype(np.float32) - high.astype(np.float32)
    middle = rest.astype(ml_dtypes.bfloat16)
    low = (rest - middle.astype(np.float32)).astype(ml_dtypes.bfloat16)
    return high, middle, low


def position_rows():
    side, quarter = SIDE // 2, D // 4
    frequency = 1.0 / 10000.0 ** (np.arange(quarter) / quarter)
    angles = np.arange(side)[:, None] * frequency[None, :]
    line = np.concatenate([np.sin(angles), np.cos(angles)], axis=1)
    parts = three_parts(line)
    zero = np.zeros_like(parts[0])
    rows = [np.concatenate([p, zero], axis=1) for p in parts]
    cols = [np.concatenate([zero, p], axis=1) for p in parts]
    return np.concatenate(rows + cols, axis=0)


def blend_tables():
    beta = 0.0001 + np.arange(TSTEPS) * (0.02 - 0.0001) / (TSTEPS - 1)
    alpha_bar = np.cumprod(1.0 - beta)
    return np.stack([np.sqrt(alpha_bar), np.sqrt(1.0 - alpha_bar)]).astype(np.float32)


def time_rates():
    steps = np.arange(128, dtype=np.float32)
    scaled = np.float32(-math.log(10000.0)) * steps / np.float32(128)
    return np.exp(scaled).astype(np.float32).reshape(1, 128)


def conv_kernel(x_ref, w_ref, msg_ref):
    taps = lax.dot_general(
        w_ref[...], x_ref[...], (((1,), (1,)), ((), ())), preferred_element_type=F32
    )
    lane = lax.broadcasted_iota(jnp.int32, (8, 128), 1)
    col = lane % SIDE
    zero = jnp.zeros((8, 128), F32)

    def tap(dy, dx, v):
        at = (dy * 3 + dx) * 8
        return taps[at : at + 8, 128 * v : 128 * v + 128]

    for v in range(8):
        rows = []
        for dy in range(3):
            left = jnp.where(col == 0, zero, pltpu.roll(tap(dy, 0, v), 1, 1))
            right = jnp.where(col == SIDE - 1, zero, pltpu.roll(tap(dy, 2, v), 127, 1))
            rows.append(left + tap(dy, 1, v) + right)
        for odd in range(2):
            parts = [pltpu.roll(r, 64, 1) if odd else r for r in rows]
            parts = [jnp.where(lane < 64, r, zero) for r in parts]
            msg_ref[2 * v + odd] = (
                parts[2] + pltpu.roll(parts[1], 32, 1) + pltpu.roll(parts[0], 64, 1)
            )


def place():
    return tuple(lax.axis_index(a) for a in ("dp_0", "dp_1", "fsdp_0", "fsdp_1"))


def gather_kernel(w1_ref, w2_ref, msg_ref, all_ref, got_ref, *sems):
    s1_send, s1_recv, s2_send, s2_recv, p_send, p_recv, m_send, m_recv = sems
    z, c, y, x = place()
    me = z * NC + c

    def x_at(k):
        return lax.rem(x + k, NX)

    def y_at(k):
        return lax.rem(y + k, NY)

    def dp_at(k):
        return lax.rem(me + k, NDP)

    def dp_device(k):
        other = dp_at(k)
        return {"dp_0": other // NC, "dp_1": lax.rem(other, NC)}

    barrier = pltpu.get_barrier_semaphore()
    for k in range(1, NX):
        pl.semaphore_signal(barrier, 1, device_id={"fsdp_1": x_at(k)}, device_id_type=MESH)
        pl.semaphore_signal(barrier, 1, device_id={"fsdp_0": y_at(k)}, device_id_type=MESH)
    for k in range(1, NDP):
        pl.semaphore_signal(barrier, 1, device_id=dp_device(k), device_id_type=MESH)
    own = jnp.where(c == 0, w1_ref[...], w2_ref[...])
    all_ref[c, y, x, 0] = own[:HALF]
    all_ref[c, y, x, 1] = own[HALF:]
    got_ref[me] = msg_ref[me]
    pl.semaphore_wait(barrier, NX - 1 + NY - 1 + NDP - 1)

    def remote(ref, at, send, recv, device):
        return pltpu.make_async_remote_copy(
            src_ref=ref.at[at],
            dst_ref=ref.at[at],
            send_sem=send,
            recv_sem=recv,
            device_id=device,
            device_id_type=MESH,
        )

    def message(k):
        return pltpu.make_async_remote_copy(
            src_ref=msg_ref.at[dp_at(k)],
            dst_ref=got_ref.at[me],
            send_sem=m_send.at[k],
            recv_sem=m_recv.at[k],
            device_id=dp_device(k),
            device_id_type=MESH,
        )

    def first(half, k):
        device = {"fsdp_1": x_at(k)} if half == 0 else {"fsdp_0": y_at(k)}
        return remote(
            all_ref, (c, y, x, half), s1_send.at[half, k], s1_recv.at[half, k], device
        )

    def line(half, k):
        if half == 0:
            return (c, y_at(NY - k), slice(None), 0)
        return (c, slice(None), x_at(NX - k), 1)

    def second(half, k):
        device = {"fsdp_0": y_at(k)} if half == 0 else {"fsdp_1": x_at(k)}
        return remote(
            all_ref, line(half, 0), s2_send.at[half, k], s2_recv.at[half, k], device
        )

    def across(half, k):
        return remote(
            all_ref, line(half, k), p_send.at[half, k], p_recv.at[half, k], {"dp_1": 1 - c}
        )

    messages = [message(k) for k in range(1, NDP)]
    firsts = [[first(h, k) for k in range(1, 4)] for h in range(2)]
    seconds = [[second(h, k) for k in range(1, 4)] for h in range(2)]
    acrosses = [[across(h, k) for k in range(4)] for h in range(2)]
    for m in messages:
        m.start()
    for k in range(3):
        for h in range(2):
            firsts[h][k].start()
    for h in range(2):
        for f in firsts[h]:
            f.wait_recv()
        for s in seconds[h]:
            s.start()
        acrosses[h][0].start()
    for k in range(3):
        for h in range(2):
            seconds[h][k].wait_recv()
            acrosses[h][k + 1].start()
    for m in messages:
        m.wait_recv()
    for h in range(2):
        for a in acrosses[h]:
            a.wait_recv()
    for group in [messages] + firsts + seconds + acrosses:
        for copy in group:
            copy.wait_send()


def split_three(value):
    high = value.astype(BF16)
    rest = value - high.astype(F32)
    middle = rest.astype(BF16)
    low = (rest - middle.astype(F32)).astype(BF16)
    return jnp.concatenate([high, middle, low], axis=0)


def joined_three(value, rows):
    return (value[2 * rows :] + value[rows : 2 * rows]) + value[:rows]


def compute_kernel(
    flips_ref,
    crops_ref,
    steps_ref,
    selected_ref,
    table_ref,
    got_ref,
    weights_ref,
    vae_ref,
    noise_ref,
    wp_ref,
    pos_ref,
    rates_ref,
    wt_ref,
    wa_ref,
    wf_ref,
    grads_ref,
    loss_ref,
    moments_ref,
    rows_ref,
    pads_ref,
    shift_ref,
    scale_ref,
    gate_ref,
    tok_ref,
    modt_ref,
    mod_ref,
    w2_ref,
    hid_ref,
    slope_ref,
    target_ref,
    gbt_ref,
    gb_ref,
    raw_ref,
    square_ref,
):
    lane = lax.broadcasted_iota(jnp.int32, (8, 128), 1)
    zero = jnp.zeros((8, 128), F32)

    for k in range(8):
        low = pltpu.roll(got_ref[2 * k], 96, 1)
        above = pltpu.roll(got_ref[2 * k + 2], 96, 1) if k < 7 else zero
        high = pltpu.roll(got_ref[2 * k + 1], 32, 1)
        below = pltpu.roll(got_ref[2 * k - 1], 32, 1) if k > 0 else zero
        four = jnp.where(lane < 96, low, above) + jnp.where(lane >= 32, high, below)
        for r in range(4):
            at = (4 * k + r) * 8
            rows_ref[at : at + 8, :] = pltpu.roll(four, 128 - 32 * r, 1) if r else four
    wide = lax.broadcasted_iota(jnp.int32, (SIDE, 128), 1) // SIDE
    halves = []
    for h in range(2):
        value = rows_ref[pl.ds(4 * h, SIDE, stride=8), :]
        for ch in range(1, 4):
            part = rows_ref[pl.ds(4 * h + ch, SIDE, stride=8), :]
            value = jnp.where(wide == ch, pltpu.roll(part, 32 * ch, 1), value)
        halves.append(value)
    by_channel = jnp.concatenate(halves, axis=1)
    source = lax.broadcasted_iota(jnp.int32, (256, 512), 0)
    goal = lax.broadcasted_iota(jnp.int32, (256, 512), 1)
    channel, column = source // SIDE, source % SIDE
    natural = column * 8 + channel
    apart = 256 + (channel // 4) * 128 + column * 4 + channel % 4
    spread = jnp.where((goal == natural) | (goal == apart), 1.0, 0.0).astype(BF16)
    placed = joined_three(
        jnp.dot(split_three(by_channel), spread, preferred_element_type=F32), SIDE
    )
    moments_ref[pl.ds(0, SIDE, stride=2), :] = placed[:, 0:128]
    moments_ref[pl.ds(1, SIDE, stride=2), :] = placed[:, 128:256]

    @pl.when(selected_ref[0, 0] != 1)
    def _():
        grads_ref[...] = jnp.zeros_like(grads_ref)
        loss_ref[...] = jnp.zeros_like(loss_ref)

    @pl.when(selected_ref[0, 0] == 1)
    def _():
        latent = placed[:, 256:384] + jnp.exp(0.5 * placed[:, 384:512]) * vae_ref[...]
        source = lax.broadcasted_iota(jnp.int32, (128, 128), 0)
        goal = lax.broadcasted_iota(jnp.int32, (128, 128), 1)
        maps = []
        for a in range(AUG):
            cell = goal // LC + crops_ref[1, a] - 2
            inside = (cell >= 0) & (cell < SIDE)
            mirror = (flips_ref[0, a] == 1).astype(jnp.int32)
            cell = cell + mirror * (SIDE - 1 - 2 * cell)
            match = inside & (source == cell * LC + goal % LC)
            maps.append(jnp.where(match, 1.0, 0.0).astype(BF16))
        columns = jnp.dot(
            split_three(latent), jnp.concatenate(maps, axis=1), preferred_element_type=F32
        )
        columns = joined_three(columns, SIDE)
        noised, noises = [], []
        for a in range(AUG):
            pads_ref[a] = jnp.zeros((40, 128), F32)
            pads_ref[a, 2 : 2 + SIDE, :] = columns[:, 128 * a : 128 * a + 128]
        for dr in range(2):
            for a in range(AUG):
                view = pads_ref[a, pl.ds(crops_ref[0, a] + dr, 16, stride=2), :]
                noise = noise_ref[pl.ds(dr * 4 + a, 16, stride=8), :]
                step = steps_ref[0, a]
                noised.append(table_ref[0, step] * view + table_ref[1, step] * noise)
                noises.append(noise)

        def patched(pieces):
            turned = jnp.concatenate(pieces, axis=0).T
            first, last = [], []
            for m in range(8):
                even = turned[16 * m : 16 * m + 8]
                odd = turned[16 * m + 8 : 16 * m + 16]
                first.append(jnp.where(lane < 64, even, pltpu.roll(odd, 64, 1)))
                last.append(jnp.where(lane < 64, pltpu.roll(even, 64, 1), odd))
            return jnp.concatenate(
                [jnp.concatenate(first, axis=1), jnp.concatenate(last, axis=1)], axis=0
            )

        patches = patched(noised).astype(BF16)
        target_ref[...] = patched(noises)

        which = lax.broadcasted_iota(jnp.int32, (96, TOK), 0)
        token = lax.broadcasted_iota(jnp.int32, (96, TOK), 1)
        cell = jnp.where(which < 48, token % 16, token // 64)
        marks = jnp.where(which % 16 == cell, 1.0, 0.0).astype(BF16)
        tok_ref[...] = lax.dot_general(
            jnp.concatenate([wp_ref[...], pos_ref[...]], axis=0),
            jnp.concatenate([patches, marks], axis=0),
            (((0,), (0,)), ((), ())),
            preferred_element_type=F32,
        )

        row = lax.broadcasted_iota(jnp.int32, (8, 128), 0)
        steps = jnp.zeros((8, 128), F32)
        for a in range(AUG):
            steps = jnp.where(row == a, steps_ref[0, a].astype(F32), steps)
        phases = steps * rates_ref[...]
        stamp = jnp.concatenate([jnp.cos(phases), jnp.sin(phases)], axis=1).astype(BF16)
        raw = jnp.dot(stamp, wt_ref[...], preferred_element_type=F32)
        conditioning = (raw * (1.0 / (1.0 + jnp.exp(-raw)))).astype(BF16)
        modulation = jnp.dot(conditioning, wa_ref[...], preferred_element_type=F32)
        views = [jnp.broadcast_to(modulation[a : a + 1], (16, 3 * D)) for a in range(AUG)]
        turned = jnp.concatenate(views + views, axis=0).T
        shift_ref[...] = turned[:D]
        scale_ref[...] = 1.0 + turned[D : 2 * D]
        gate_ref[...] = turned[2 * D :]

        @pl.loop(0, TOK // 128)
        def _(m):
            at = pl.ds(pl.multiple_of(m * 128, 128), 128)
            value = tok_ref[:, at]
            center = value - jnp.sum(value, axis=0, keepdims=True) * (1.0 / D)
            variance = jnp.sum(center * center, axis=0, keepdims=True) * (1.0 / D)
            normed = center * lax.rsqrt(variance + norm_epsilon)
            out = normed * scale_ref[...] + shift_ref[...]
            modt_ref[:, at] = out.astype(BF16)
            mod_ref[at, :] = out.T.astype(BF16)

        @pl.loop(0, FF // 128)
        def _(m):
            at = pl.ds(pl.multiple_of(m * 128, 128), 128)
            w2_ref[:, at] = weights_ref[1, at, :].astype(F32).T.astype(BF16)

        root = math.sqrt(2.0 / math.pi)

        @pl.loop(0, FF // CHUNK)
        def _(f):
            at = pl.ds(pl.multiple_of(f * CHUNK, CHUNK), CHUNK)
            pre = jnp.dot(weights_ref[0, at, :], modt_ref[...], preferred_element_type=F32)
            squared = pre * pre
            inner = pre * (squared * (root * 0.044715) + root)
            share = 0.5 * jnp.tanh(inner) + 0.5
            hidden = pre * share
            hid_ref[at, :] = hidden.astype(BF16)
            slope = (1.0 - share) * hidden * (squared * (6.0 * root * 0.044715) + 2.0 * root)
            slope_ref[at, :] = slope + share

        loss_ref[...] = jnp.zeros_like(loss_ref)

        @pl.loop(0, TOK // 256)
        def _(m):
            at = pl.ds(pl.multiple_of(m * 256, 256), 256)
            branch = jnp.dot(w2_ref[...], hid_ref[:, at], preferred_element_type=F32)
            gate = jnp.concatenate([gate_ref[...], gate_ref[...]], axis=1)
            mixed = tok_ref[:, at] + gate * branch
            center = mixed - jnp.sum(mixed, axis=0, keepdims=True) * (1.0 / D)
            variance = jnp.sum(center * center, axis=0, keepdims=True) * (1.0 / D)
            inverse = lax.rsqrt(variance + norm_epsilon)
            normed = center * inverse
            predicted = jnp.dot(wf_ref[...], normed.astype(BF16), preferred_element_type=F32)
            residue = predicted - target_ref[:, at]
            loss_ref[...] += jnp.sum(residue * residue) * (1.0 / (TOK * 16))
            grad_pred = (residue * (2.0 / (TOK * 16))).astype(BF16)
            grad_normed = lax.dot_general(
                wf_ref[...], grad_pred, (((0,), (0,)), ((), ())), preferred_element_type=F32
            )
            mean = jnp.sum(grad_normed, axis=0, keepdims=True) * (1.0 / D)
            along = jnp.sum(grad_normed * normed, axis=0, keepdims=True) * (1.0 / D)
            grad_mixed = inverse * (grad_normed - mean - normed * along)
            grad_branch = gate * grad_mixed
            gbt_ref[:, at] = grad_branch.astype(BF16)
            gb_ref[at, :] = grad_branch.T.astype(BF16)

        square_ref[...] = jnp.zeros_like(square_ref)

        @pl.loop(0, FF // CHUNK)
        def _(f):
            at = pl.ds(pl.multiple_of(f * CHUNK, CHUNK), CHUNK)
            grad_hidden = jnp.dot(
                weights_ref[1, at, :], gbt_ref[...], preferred_element_type=F32
            )
            grad_pre = (slope_ref[at, :] * grad_hidden).astype(BF16)
            grad_1 = jnp.dot(grad_pre, mod_ref[...], preferred_element_type=F32)
            grad_2 = jnp.dot(hid_ref[at, :], gb_ref[...], preferred_element_type=F32)
            raw_ref[0, at, :] = grad_1
            raw_ref[1, at, :] = grad_2
            square_ref[...] += jnp.sum(
                grad_1 * grad_1 + grad_2 * grad_2, axis=0, keepdims=True
            )

        total = jnp.sum(square_ref[...], axis=1, keepdims=True)
        factor = 1.0 / (jnp.sqrt(total * (1.0 / (2 * D * FF))) + clip_offset)

        @pl.loop(0, FF // CHUNK)
        def _(f):
            at = pl.ds(pl.multiple_of(f * CHUNK, CHUNK), CHUNK)
            for w in range(2):
                grads_ref[w, at, :] = (raw_ref[w, at, :] * factor).astype(BF16)


def reduce_kernel(g_ref, loss_ref, sum_ref, total_ref, *scratch):
    (r0, s1, r1, acc, r2, tiles, r3, whole, l0, l1, l2) = scratch[:11]
    (q_send, q_recv, s1_send, s1_recv, s2_send, s2_recv, z_send, z_recv) = scratch[11:19]
    (a_send, a_recv, f_send, f_recv, l_send, l_recv) = scratch[19:]
    z, c, y, x = place()
    partner = {"dp_1": 1 - c}

    def x_at(k):
        return lax.rem(x + k, NX)

    def y_at(k):
        return lax.rem(y + k, NY)

    def z_at(k):
        return lax.rem(z + k, NZ)

    barrier = pltpu.get_barrier_semaphore()
    pl.semaphore_signal(barrier, 1, device_id=partner, device_id_type=MESH)
    for k in range(1, NX):
        pl.semaphore_signal(barrier, 1, device_id={"fsdp_1": x_at(k)}, device_id_type=MESH)
        pl.semaphore_signal(barrier, 1, device_id={"fsdp_0": y_at(k)}, device_id_type=MESH)
    for k in range(1, NZ):
        pl.semaphore_signal(barrier, 1, device_id={"dp_0": z_at(k)}, device_id_type=MESH)
    l0[0] = loss_ref[...]
    pl.semaphore_wait(barrier, 1 + NX - 1 + NY - 1 + NZ - 1)

    def remote(src, dst, send, recv, device):
        return pltpu.make_async_remote_copy(
            src_ref=src,
            dst_ref=dst,
            send_sem=send,
            recv_sem=recv,
            device_id=device,
            device_id_type=MESH,
        )

    def piece(half, k):
        if half == 0:
            return (slice(None), x_at(k), 0)
        return (y_at(k), slice(None), 1)

    def part(half, k, j):
        if half == 0:
            return (j, x_at(k), 0)
        return (y_at(k), j, 1)

    def first_to(half, k):
        return {"fsdp_1": x_at(k)} if half == 0 else {"fsdp_0": y_at(k)}

    def second_to(half, k):
        return {"fsdp_0": y_at(k)} if half == 0 else {"fsdp_1": x_at(k)}

    def second_at(half, k):
        return y_at(k) if half == 0 else x_at(k)

    loss_0 = remote(l0.at[0], l0.at[1], l_send.at[0], l_recv.at[0], partner)
    loss_0.start()
    swaps = {}
    for k in (2, 1, 3, 0):
        for h in range(2):
            at = piece(h, k)
            swaps[h, k] = remote(
                g_ref.at[(1 - c,) + at], r0.at[at], q_send.at[h, k], q_recv.at[h, k], partner
            )
            swaps[h, k].start()
    firsts = {}
    for k in (2, 1, 3, 0):
        for h in range(2):
            swaps[h, k].wait_recv()
            for j in range(4):
                at = part(h, k, j)
                value = g_ref[(c,) + at].astype(F32) + r0[at].astype(F32)
                if k == 0:
                    acc[h, j] = value
                else:
                    s1[h, k - 1, j] = value.astype(BF16)
            if k > 0:
                firsts[h, k] = remote(
                    s1.at[h, k - 1],
                    r1.at[h, k - 1],
                    s1_send.at[h, k],
                    s1_recv.at[h, k],
                    first_to(h, k),
                )
                firsts[h, k].start()
    loss_0.wait_recv()
    l1[x] = l0[0] + l0[1]
    losses = [loss_0]
    for k in range(1, NX):
        copy = remote(l1.at[x], l1.at[x], l_send.at[k], l_recv.at[k], {"fsdp_1": x_at(k)})
        copy.start()
        losses.append(copy)
    seconds = {}
    for h in range(2):
        for k in (1, 3, 2):
            firsts[h, k].wait_recv()
        for k in (2, 1, 3, 0):
            j = second_at(h, k)
            acc[h, j] = (acc[h, j] + r1[h, 0, j].astype(F32)) + (
                r1[h, 1, j].astype(F32) + r1[h, 2, j].astype(F32)
            )
            if k > 0:
                seconds[h, k] = remote(
                    acc.at[h, j],
                    r2.at[h, k - 1],
                    s2_send.at[h, k],
                    s2_recv.at[h, k],
                    second_to(h, k),
                )
                seconds[h, k].start()
    for copy in losses[1:]:
        copy.wait_recv()
    l2[y] = (l1[0] + l1[1]) + (l1[2] + l1[3])
    for k in range(1, NY):
        copy = remote(
            l2.at[y], l2.at[y], l_send.at[3 + k], l_recv.at[3 + k], {"fsdp_0": y_at(k)}
        )
        copy.start()
        losses.append(copy)
    for h in range(2):
        for k in (1, 3, 2):
            seconds[h, k].wait_recv()
        j = second_at(h, 0)
        value = (acc[h, j] + r2[h, 0]) + (r2[h, 1] + r2[h, 2])
        for i in range(HALF // 8):
            for n in range(D // 128):
                t = (h * (HALF // 8) + i) * (D // 128) + n
                tiles[t // PIECE, t % PIECE] = value[8 * i : 8 * i + 8, 128 * n : 128 * n + 128]
    for copy in losses[4:]:
        copy.wait_recv()
    at = USED_TILES
    tiles[at // PIECE, at % PIECE] = (l2[0] + l2[1]) + (l2[2] + l2[3])
    for t in range(USED_TILES + 1, TILES):
        tiles[t // PIECE, t % PIECE] = jnp.zeros((8, 128), F32)

    order = (4, 3, 5, 2, 6, 1, 7)
    thirds = []
    for k in order:
        copy = remote(
            tiles.at[z_at(k)], r3.at[z], z_send.at[k], z_recv.at[k], {"dp_0": z_at(k)}
        )
        copy.start()
        thirds.append(copy)
    r3[z] = tiles[z]
    for copy in thirds:
        copy.wait_recv()
    value = r3[0]
    for k in range(1, NZ):
        value = value + r3[k]
    whole[c, z] = value
    spreads = {}
    for k in order:
        spreads[k] = remote(
            whole.at[c, z], whole.at[c, z], a_send.at[k], a_recv.at[k], {"dp_0": z_at(k)}
        )
        spreads[k].start()
    crossings = []
    for k in (0, 7, 1, 6, 2, 5, 3, 4):
        if k > 0:
            spreads[k].wait_recv()
        at = z_at(NZ - k) if k > 0 else z
        copy = remote(whole.at[c, at], whole.at[c, at], f_send.at[k], f_recv.at[k], partner)
        copy.start()
        crossings.append(copy)
    for copy in crossings:
        copy.wait_recv()
    for w in range(2):
        for t in range(USED_TILES):
            i, n = t // (D // 128), t % (D // 128)
            sum_ref[w, 8 * i : 8 * i + 8, 128 * n : 128 * n + 128] = whole[
                w, t // PIECE, t % PIECE
            ]
    total_ref[...] = whole[0, USED_TILES // PIECE, USED_TILES % PIECE]
    for group in (swaps, firsts, seconds, spreads):
        for copy in group.values():
            copy.wait_send()
    for group in (losses, thirds, crossings):
        for copy in group:
            copy.wait_send()


def per_device(
    features,
    conv_weight,
    vae_noise,
    flips,
    crops,
    tsteps,
    diffusion_noise,
    selected,
    w_patch,
    w_time,
    w_ada,
    w_fc1,
    w_fc2,
    w_final,
    noise_fc1,
    noise_fc2,
):
    dma = pltpu.SemaphoreType.DMA
    pixels = features.reshape(TOK, FCH)
    taps = conv_weight.transpose(0, 1, 3, 2).reshape(72, FCH)
    messages = pl.pallas_call(
        conv_kernel,
        out_shape=jax.ShapeDtypeStruct((NDP, 8, 128), F32),
        in_specs=[VMEM_SPEC] * 2,
        out_specs=VMEM_SPEC,
        name="conv",
    )(pixels, taps)
    gathered, received = pl.pallas_call(
        gather_kernel,
        out_shape=(
            jax.ShapeDtypeStruct((2, NY, NX, 2, HALF, D), BF16),
            jax.ShapeDtypeStruct((NDP, 8, 128), F32),
        ),
        in_specs=[VMEM_SPEC] * 3,
        out_specs=(VMEM_SPEC, VMEM_SPEC),
        scratch_shapes=[dma((2, 4))] * 6 + [dma((NDP,))] * 2,
        compiler_params=pltpu.CompilerParams(collective_id=0, has_side_effects=True),
        name="gather",
    )(w_fc1.T, w_fc2.T, messages)
    weights = gathered.reshape(2, FF, D)
    views = diffusion_noise.reshape(AUG, SIDE, SIDE * LC).transpose(1, 0, 2)
    grads, loss, moments = pl.pallas_call(
        compute_kernel,
        out_shape=(
            jax.ShapeDtypeStruct((2, FF, D), BF16),
            jax.ShapeDtypeStruct((8, 128), F32),
            jax.ShapeDtypeStruct((2 * SIDE, 128), F32),
        ),
        in_specs=[SMEM_SPEC] * 5 + [VMEM_SPEC] * 10,
        out_specs=(VMEM_SPEC,) * 3,
        scratch_shapes=[
            pltpu.VMEM((256, 128), F32),
            pltpu.VMEM((AUG, 40, 128), F32),
            pltpu.VMEM((D, 128), F32),
            pltpu.VMEM((D, 128), F32),
            pltpu.VMEM((D, 128), F32),
            pltpu.VMEM((D, TOK), F32),
            pltpu.VMEM((D, TOK), BF16),
            pltpu.VMEM((TOK, D), BF16),
            pltpu.VMEM((D, FF), BF16),
            pltpu.VMEM((FF, TOK), BF16),
            pltpu.VMEM((FF, TOK), F32),
            pltpu.VMEM((16, TOK), F32),
            pltpu.VMEM((D, TOK), BF16),
            pltpu.VMEM((TOK, D), BF16),
            pltpu.VMEM((2, FF, D), F32),
            pltpu.VMEM((1, D), F32),
        ],
        compiler_params=pltpu.CompilerParams(vmem_limit_bytes=56 << 20),
        name="example",
    )(
        flips.reshape(1, AUG),
        crops.reshape(AUG, 2).T,
        tsteps.reshape(1, AUG),
        selected,
        jnp.asarray(blend_tables()),
        received,
        weights,
        vae_noise.reshape(SIDE, SIDE * LC),
        views.reshape(SIDE * AUG, SIDE * LC),
        w_patch,
        jnp.asarray(position_rows()),
        jnp.asarray(time_rates()),
        w_time,
        w_ada,
        w_final.T,
    )
    quarter = (2, 4, HALF, D)
    sums, total = pl.pallas_call(
        reduce_kernel,
        out_shape=(
            jax.ShapeDtypeStruct((2, SHARD, D), F32),
            jax.ShapeDtypeStruct((8, 128), F32),
        ),
        in_specs=[VMEM_SPEC] * 2,
        out_specs=(VMEM_SPEC, VMEM_SPEC),
        scratch_shapes=[
            pltpu.VMEM((NY, NX, 2, HALF, D), BF16),
            pltpu.VMEM((2, 3, 4, HALF, D), BF16),
            pltpu.VMEM((2, 3, 4, HALF, D), BF16),
            pltpu.VMEM(quarter, F32),
            pltpu.VMEM((2, 3, HALF, D), F32),
            pltpu.VMEM((NZ, PIECE, 8, 128), F32),
            pltpu.VMEM((NZ, PIECE, 8, 128), F32),
            pltpu.VMEM((2, NZ, PIECE, 8, 128), F32),
            pltpu.VMEM((2, 8, 128), F32),
            pltpu.VMEM((NX, 8, 128), F32),
            pltpu.VMEM((NY, 8, 128), F32),
        ]
        + [dma((2, 4))] * 6
        + [dma((NZ,))] * 8,
        compiler_params=pltpu.CompilerParams(collective_id=1, has_side_effects=True),
        name="reduce",
    )(grads.reshape(2, NY, NX, 2, HALF, D), loss)
    update_fc1 = (sums[0].T + noise_weight * noise_fc1) / SELECTED
    update_fc2 = (sums[1].T + noise_weight * noise_fc2) / SELECTED
    return (update_fc1, update_fc2, total[0, 0] / SELECTED, moments.reshape(1, 1, -1))


def solution(mesh):
    split = Mesh(mesh.devices.reshape(NZ, NC, NY, NX), DP + FSDP)
    return jax.shard_map(
        per_device,
        mesh=split,
        in_specs=(
            P(FSDP, None, DP, None, None),
            P(),
            P(DP, FSDP, None),
            P(DP, FSDP, None),
            P(DP, FSDP, None, None),
            P(DP, FSDP, None),
            P(DP, FSDP, None, None),
            P(DP, FSDP),
            P(),
            P(),
            P(),
            P(None, FSDP),
            P(None, FSDP),
            P(),
            P(None, FSDP),
            P(None, FSDP),
        ),
        out_specs=(P(None, FSDP), P(None, FSDP), P(), P(DP, FSDP, None)),
        check_vma=False,
    )
```

time: 372 us -> 95.1 us (0.26)
  waiting for transfers between devices: 182 us -> 0 us
  Pallas kernels: 0 us -> 88.8 us
  local copies, waits for them, and re-layouts: 67.3 us -> 1.2 us
  blocking collectives: 39.6 us -> 0 us
  matrix products: 25.8 us -> 0 us
  other arithmetic: 20 us -> 1.73 us
  starting transfers between devices: 17.3 us -> 0 us
  between operations: 16.4 us -> 3.11 us
    pallas_call x0 -> x4, Pallas kernels: none -> 88.8 us  [the longest x1 34.1 us: per_device(): pl.pallas_call(reduce_kernel, out_shape=(jax.ShapeDtypeStruct((2, SHARD,...]
    reduce_scatter x1 -> x0, waiting for transfers between devices: 82.4 us -> none  [one_scatter(): lax.psum_scatter(lines, axis, tiled=True).reshape(-1)]
    psum x1 -> x0, waiting for transfers between devices: 65.8 us -> none  [together(): total = lax.psum(jnp.concatenate([a.ravel() for a in arrays]), axis)]
    psum x4 -> x0, blocking collectives: 39.6 us -> none  [over_axes(): return functools.reduce(lax.psum, axes, value)]
    all_gather x1 -> x0, waiting for transfers between devices: 33.4 us -> none  [turned_gather(): whole = lax.all_gather(both, axis, axis=0, tiled=True)]
    dot_general x9 -> x0, matrix products: 25.8 us -> none  [the longest x1 11.1 us: example_terms(): lax.dot_general(modulated, grad_pre, (((0,), (0,)), ((), ())), preferred_...]
    reshape x6 -> x0, local copies, waits for them, and re-layouts: 14.7 us -> none  [the longest x2 8.63 us: one_scatter(): lines = jnp.concatenate([b.reshape(length, -1) for b in tiles], axis=1)]
    cond x40 -> x0, local copies, waits for them, and re-layouts: 12.7 us -> none
  transfers between devices with their start and end apart: 6 -> 0, of which waited for: 4 -> 0; matrix products, arithmetic and copies ran while one was open for 2% -> 0% of each run, Pallas kernels for 0% -> 0%
where the time goes in v1:
time: 95.1 us; the launch traced here: 94.9 us
  Pallas kernels  88.8 us (93%)
  between operations  3.11 us (3%)
  other arithmetic  1.73 us (2%)
  local copies, waits for them, and re-layouts  1.2 us (1%)
    pallas_call x1, Pallas kernels, per_device(): pl.pallas_call(reduce_kernel, out_shape=(jax.ShapeDtypeStruct((2, SHARD,...  34.1 us
    pallas_call x1, Pallas kernels, per_device(): pl.pallas_call(gather_kernel, out_shape=(jax.ShapeDtypeStruct((2, NY, NX,...  28.7 us
    pallas_call x1, Pallas kernels, per_device(): pl.pallas_call(compute_kernel, out_shape=(jax.ShapeDtypeStruct((2, FF, D)...  23.6 us
    pallas_call x1, Pallas kernels, per_device(): pl.pallas_call(conv_kernel, out_shape=jax.ShapeDtypeStruct((NDP, 8, 128),...  2.54 us

profile of v1, /device:TPU:1, one launch (start us, length us, event | category | flops | bytes accessed | tf_op | source)
XLA Modules:
  0.0 94.9 jit_solution(11565780536128740154)
XLA Ops:
  1.3 2.5 %conv.1.msg_ref = f32[16,8,128]{2,1,0:T(8,128)} custom-call(bf16[1024,512]{1,0:T(8,128)(2,1)} %bitcast.36, bf16[72,512]{1,0:T(8,128)(2,1)} %bitcast.37), custom_call_target="tpu_custom_call" | custom-call | tf_op jit(solution)/shard_map/conv/pallas_call | solution.py:639
  3.8 28.7 %gather.1 = (bf16[2,4,4,2,48,384]{5,4,3,2,1,0:T(8,128)(2,1)}, f32[16,8,128]{2,1,0:T(8,128)}) custom-call(bf16[96,384]{1,0:T(8,128)(2,1)} %bitcast.38, bf16[96,384]{1,0:T(8,128)(2,1)} %bitcast.39, f32[16,8,128]{2,1,0:T(8,128)} %conv.1.msg_ref), custom_call_target="tpu_custom_call" | custom-call | tf_op jit(solution)/shard_map/gather/pallas_call | solution.py:646
  32.5 0.0 copy-start
  32.5 0.0 copy-start.1
  32.5 23.6 %example.1 = (bf16[2,1536,384]{2,1,0:T(8,128)(2,1)}, f32[8,128]{1,0:T(8,128)}, f32[64,128]{1,0:T(8,128)}) custom-call(s32[1,4]{1,0:T(1,128)} %bitcast.44, s32[2,4]{1,0:T(2,128)} %bitcast.43, s32[1,4]{1,0:T(1,128)} %bitcast.45, s32[1,1]{1,0:T(1,128)S(6)} %copy.24.selected_ref, f32[2,1000]{1,0:T(2,128)} %constant.16.clone.table_ref, ...), custom_call_target="tpu_custom_call" | custom-call | tf_op jit(solution)/shard_map/example/pallas_call | solution.py:660
  56.1 34.1 %reduce.1 = (f32[2,96,384]{2,1,0:T(8,128)}, f32[8,128]{1,0:T(8,128)}) custom-call(bf16[2,4,4,2,48,384]{5,4,3,2,1,0:T(8,128)(2,1)} %bitcast.34, f32[8,128]{1,0:T(8,128)} %get-tuple-element.14.loss_ref), custom_call_target="tpu_custom_call" | custom-call | tf_op jit(solution)/shard_map/reduce/pallas_call | solution.py:707
  90.2 1.2 %slice.11 = f32[1,1]{1,0:T(1,128)} slice(f32[8,128]{1,0:T(8,128)} %get-tuple-element.16), slice={[0:1], [0:1]} | slice | bytes 8 | tf_op jit(solution)/shard_map/slice | solution.py:735
  92.0 0.0 copy-done
  92.0 0.0 copy-done.1
  92.0 1.7 %fusion = (f32[384,96]{0,1:T(8,128)}, f32[384,96]{0,1:T(8,128)}) fusion(f32[384,96]{0,1:T(8,128)S(1)} %copy-done, f32[2,96,384]{2,1,0:T(8,128)} %get-tuple-element.15, f32[384,96]{0,1:T(8,128)S(1)} %copy-done.1), kind=kLoop, calls=%fused_computation.1 | loop fusion | flops 221184 | bytes 884736 | tf_op jit(solution)/shard_map/div | solution.py:734
Async XLA Ops:
  32.5 59.5 %copy-start = (f32[384,96]{0,1:T(8,128)S(1)}, f32[384,96]{0,1:T(8,128)}, u32[]{:S(2)}) copy-start(f32[384,96]{0,1:T(8,128)} %param.34) | copy-start | bytes 442372
  32.5 59.5 %copy-start.1 = (f32[384,96]{0,1:T(8,128)S(1)}, f32[384,96]{0,1:T(8,128)}, u32[]{:S(2)}) copy-start(f32[384,96]{0,1:T(8,128)} %param.33) | copy-start | bytes 442372

commit v2 on v1

--- a/solution.py
+++ b/solution.py
@@ -155,10 +155,23 @@
             return (c, y_at(NY - k), slice(None), 0)
         return (c, slice(None), x_at(NX - k), 1)
 
-    def second(half, k):
-        device = {"fsdp_0": y_at(k)} if half == 0 else {"fsdp_1": x_at(k)}
+    def half_line(half, k, part):
+        at = pl.ds(2 * part, 2)
+        if half == 0:
+            return (c, y_at(NY - k), at, 0)
+        return (c, at, x_at(NX - k), 1)
+
+    def second(half, slot):
+        up = slot < 3
+        k, part = ((0, 0), (0, 1), (1, 0), (0, 1), (0, 0), (3, 1))[slot]
+        step = 1 if up else 3
+        device = {"fsdp_0": y_at(step)} if half == 0 else {"fsdp_1": x_at(step)}
         return remote(
-            all_ref, line(half, 0), s2_send.at[half, k], s2_recv.at[half, k], device
+            all_ref,
+            half_line(half, k, part),
+            s2_send.at[half, slot],
+            s2_recv.at[half, slot],
+            device,
         )
 
     def across(half, k):
@@ -168,23 +181,31 @@
 
     messages = [message(k) for k in range(1, NDP)]
     firsts = [[first(h, k) for k in range(1, 4)] for h in range(2)]
-    seconds = [[second(h, k) for k in range(1, 4)] for h in range(2)]
+    seconds = [[second(h, slot) for slot in range(6)] for h in range(2)]
     acrosses = [[across(h, k) for k in range(4)] for h in range(2)]
     for m in messages:
         m.start()
-    for k in range(3):
+    for k in (1, 0, 2):
         for h in range(2):
             firsts[h][k].start()
     for h in range(2):
         for f in firsts[h]:
             f.wait_recv()
-        for s in seconds[h]:
-            s.start()
+        for slot in (0, 3, 1, 4):
+            seconds[h][slot].start()
         acrosses[h][0].start()
-    for k in range(3):
+    for slot in (0, 3):
         for h in range(2):
-            seconds[h][k].wait_recv()
-            acrosses[h][k + 1].start()
+            seconds[h][slot].wait_recv()
+            seconds[h][slot + 2].start()
+    for slot in (1, 4):
+        for h in range(2):
+            seconds[h][slot].wait_recv()
+            acrosses[h][1 if slot == 1 else 3].start()
+    for h in range(2):
+        seconds[h][2].wait_recv()
+        seconds[h][5].wait_recv()
+        acrosses[h][2].start()
     for m in messages:
         m.wait_recv()
     for h in range(2):
@@ -435,9 +456,9 @@
 
 
 def reduce_kernel(g_ref, loss_ref, sum_ref, total_ref, *scratch):
-    (r0, s1, r1, acc, r2, tiles, r3, whole, l0, l1, l2) = scratch[:11]
-    (q_send, q_recv, s1_send, s1_recv, s2_send, s2_recv, z_send, z_recv) = scratch[11:19]
-    (a_send, a_recv, f_send, f_recv, l_send, l_recv) = scratch[19:]
+    (r0, s1, r1, acc, c2, r2, tiles, r3, whole, l0, l1, l2) = scratch[:12]
+    (q_send, q_recv, s1_send, s1_recv, s2_send, s2_recv, z_send, z_recv) = scratch[12:20]
+    (a_send, a_recv, f_send, f_recv, l_send, l_recv) = scratch[20:]
     z, c, y, x = place()
     partner = {"dp_1": 1 - c}
 
@@ -500,25 +521,44 @@
             )
             swaps[h, k].start()
     firsts = {}
-    for k in (2, 1, 3, 0):
+
+    def first(h, slot, src):
+        firsts[h, slot] = remote(
+            src,
+            r1.at[h, slot],
+            s1_send.at[h, slot],
+            s1_recv.at[h, slot],
+            first_to(h, 1 if slot < 3 else 3),
+        )
+        firsts[h, slot].start()
+
+    def own(h, k, j):
+        at = part(h, k, j)
+        return g_ref[(c,) + at].astype(F32) + r0[at].astype(F32)
+
+    for h in range(2):
+        swaps[h, 2].wait_recv()
+        for j in range(4):
+            s1[h, 1, j] = own(h, 2, j).astype(BF16)
+        first(h, 0, s1.at[h, 1, pl.ds(0, 2)])
+        first(h, 3, s1.at[h, 1, pl.ds(2, 2)])
+    for k, slot, low in ((1, 1, 2), (3, 4, 0)):
         for h in range(2):
             swaps[h, k].wait_recv()
-            for j in range(4):
-                at = part(h, k, j)
-                value = g_ref[(c,) + at].astype(F32) + r0[at].astype(F32)
-                if k == 0:
-                    acc[h, j] = value
-                else:
-                    s1[h, k - 1, j] = value.astype(BF16)
-            if k > 0:
-                firsts[h, k] = remote(
-                    s1.at[h, k - 1],
-                    r1.at[h, k - 1],
-                    s1_send.at[h, k],
-                    s1_recv.at[h, k],
-                    first_to(h, k),
-                )
-                firsts[h, k].start()
+            for j in (low, low + 1):
+                s1[h, k - 1, j] = own(h, k, j).astype(BF16)
+            first(h, slot, s1.at[h, k - 1, pl.ds(low, 2)])
+    for k, slot, low in ((1, 0, 0), (3, 3, 2)):
+        for h in range(2):
+            firsts[h, slot].wait_recv()
+            for i in range(2):
+                j = low + i
+                s1[h, k - 1, j] = (own(h, k, j) + r1[h, slot, i].astype(F32)).astype(BF16)
+            first(h, slot + 2, s1.at[h, k - 1, pl.ds(low, 2)])
+    for h in range(2):
+        swaps[h, 0].wait_recv()
+        for j in range(4):
+            acc[h, j] = own(h, 0, j)
     loss_0.wait_recv()
     l1[x] = l0[0] + l0[1]
     losses = [loss_0]
@@ -527,23 +567,32 @@
         copy.start()
         losses.append(copy)
     seconds = {}
+    quarter = HALF // 2
+
+    def second(h, slot, src):
+        seconds[h, slot] = remote(
+            src,
+            r2.at[h, slot],
+            s2_send.at[h, slot],
+            s2_recv.at[h, slot],
+            second_to(h, 1 if slot < 3 else 3),
+        )
+        seconds[h, slot].start()
+
+    def rows(part):
+        return pl.ds(part * quarter, quarter)
+
     for h in range(2):
-        for k in (1, 3, 2):
-            firsts[h, k].wait_recv()
-        for k in (2, 1, 3, 0):
-            j = second_at(h, k)
-            acc[h, j] = (acc[h, j] + r1[h, 0, j].astype(F32)) + (
-                r1[h, 1, j].astype(F32) + r1[h, 2, j].astype(F32)
-            )
-            if k > 0:
-                seconds[h, k] = remote(
-                    acc.at[h, j],
-                    r2.at[h, k - 1],
-                    s2_send.at[h, k],
-                    s2_recv.at[h, k],
-                    second_to(h, k),
-                )
-                seconds[h, k].start()
+        for slot in (4, 1, 2, 5):
+            firsts[h, slot].wait_recv()
+        for j in range(4):
+            a, b = (2, 4) if j < 2 else (1, 5)
+            acc[h, j] += r1[h, a, j % 2].astype(F32) + r1[h, b, j % 2].astype(F32)
+        far, up, down = second_at(h, 2), second_at(h, 1), second_at(h, 3)
+        second(h, 0, acc.at[h, far, rows(0)])
+        second(h, 3, acc.at[h, far, rows(1)])
+        second(h, 1, acc.at[h, up, rows(1)])
+        second(h, 4, acc.at[h, down, rows(0)])
     for copy in losses[1:]:
         copy.wait_recv()
     l2[y] = (l1[0] + l1[1]) + (l1[2] + l1[3])
@@ -553,11 +602,22 @@
         )
         copy.start()
         losses.append(copy)
+    for slot, k, side in ((0, 1, 0), (3, 3, 1)):
+        for h in range(2):
+            seconds[h, slot].wait_recv()
+            c2[h, side] = acc[h, second_at(h, k), rows(side), :] + r2[h, slot]
+            second(h, slot + 2, c2.at[h, side])
     for h in range(2):
-        for k in (1, 3, 2):
-            seconds[h, k].wait_recv()
+        for slot in (1, 4, 2, 5):
+            seconds[h, slot].wait_recv()
         j = second_at(h, 0)
-        value = (acc[h, j] + r2[h, 0]) + (r2[h, 1] + r2[h, 2])
+        value = jnp.concatenate(
+            [
+                acc[h, j, rows(0), :] + (r2[h, 2] + r2[h, 4]),
+                acc[h, j, rows(1), :] + (r2[h, 1] + r2[h, 5]),
+            ],
+            axis=0,
+        )
         for i in range(HALF // 8):
             for n in range(D // 128):
                 t = (h * (HALF // 8) + i) * (D // 128) + n
@@ -613,6 +673,12 @@
     for group in (losses, thirds, crossings):
         for copy in group:
             copy.wait_send()
+
+
+def finish_kernel(sum_ref, total_ref, n1_ref, n2_ref, u1_ref, u2_ref, mean_ref):
+    u1_ref[...] = (sum_ref[0] + noise_weight * n1_ref[...]) * (1.0 / SELECTED)
+    u2_ref[...] = (sum_ref[1] + noise_weight * n2_ref[...]) * (1.0 / SELECTED)
+    mean_ref[...] = total_ref[0:1, 0:1] * (1.0 / SELECTED)
 
 
 def per_device(
@@ -651,7 +717,10 @@
         ),
         in_specs=[VMEM_SPEC] * 3,
         out_specs=(VMEM_SPEC, VMEM_SPEC),
-        scratch_shapes=[dma((2, 4))] * 6 + [dma((NDP,))] * 2,
+        scratch_shapes=[dma((2, 4))] * 2
+        + [dma((2, 6))] * 2
+        + [dma((2, 4))] * 2
+        + [dma((NDP,))] * 2,
         compiler_params=pltpu.CompilerParams(collective_id=0, has_side_effects=True),
         name="gather",
     )(w_fc1.T, w_fc2.T, messages)
@@ -703,7 +772,6 @@
         w_ada,
         w_final.T,
     )
-    quarter = (2, 4, HALF, D)
     sums, total = pl.pallas_call(
         reduce_kernel,
         out_shape=(
@@ -715,9 +783,10 @@
         scratch_shapes=[
             pltpu.VMEM((NY, NX, 2, HALF, D), BF16),
             pltpu.VMEM((2, 3, 4, HALF, D), BF16),
-            pltpu.VMEM((2, 3, 4, HALF, D), BF16),
-            pltpu.VMEM(quarter, F32),
-            pltpu.VMEM((2, 3, HALF, D), F32),
+            pltpu.VMEM((2, 6, 2, HALF, D), BF16),
+            pltpu.VMEM((2, 4, HALF, D), F32),
+            pltpu.VMEM((2, 2, HALF // 2, D), F32),
+            pltpu.VMEM((2, 6, HALF // 2, D), F32),
             pltpu.VMEM((NZ, PIECE, 8, 128), F32),
             pltpu.VMEM((NZ, PIECE, 8, 128), F32),
             pltpu.VMEM((2, NZ, PIECE, 8, 128), F32),
@@ -725,14 +794,24 @@
             pltpu.VMEM((NX, 8, 128), F32),
             pltpu.VMEM((NY, 8, 128), F32),
         ]
-        + [dma((2, 4))] * 6
+        + [dma((2, 4))] * 2
+        + [dma((2, 6))] * 4
         + [dma((NZ,))] * 8,
         compiler_params=pltpu.CompilerParams(collective_id=1, has_side_effects=True),
         name="reduce",
     )(grads.reshape(2, NY, NX, 2, HALF, D), loss)
-    update_fc1 = (sums[0].T + noise_weight * noise_fc1) / SELECTED
-    update_fc2 = (sums[1].T + noise_weight * noise_fc2) / SELECTED
-    return (update_fc1, update_fc2, total[0, 0] / SELECTED, moments.reshape(1, 1, -1))
+    update_1, update_2, mean_loss = pl.pallas_call(
+        finish_kernel,
+        out_shape=(
+            jax.ShapeDtypeStruct((SHARD, D), F32),
+            jax.ShapeDtypeStruct((SHARD, D), F32),
+            jax.ShapeDtypeStruct((1, 1), F32),
+        ),
+        in_specs=[VMEM_SPEC] * 4,
+        out_specs=(VMEM_SPEC,) * 3,
+        name="finish",
+    )(sums, total, noise_fc1.T, noise_fc2.T)
+    return (update_1.T, update_2.T, mean_loss.reshape(()), moments.reshape(1, 1, -1))
 
 
 def solution(mesh):

time: 95.1 us -> 91.6 us (0.963)
  between operations: 3.11 us -> 1.29 us
  other arithmetic: 1.73 us -> 0 us
  Pallas kernels: 88.8 us -> 90 us
  local copies, waits for them, and re-layouts: 1.2 us -> 0 us
    pallas_call x1, Pallas kernels: 34.1 us -> 54.1 us  [per_device(): pl.pallas_call(reduce_kernel, out_shape=(jax.ShapeDtypeStruct((2, SHARD,...]
    pallas_call x1, Pallas kernels: 23.6 us -> 3.99 us  [per_device(): pl.pallas_call(compute_kernel, out_shape=(jax.ShapeDtypeStruct((2, FF, D)...]
    pallas_call x0 -> x1, Pallas kernels: none -> 1.82 us  [per_device(): pl.pallas_call(finish_kernel, out_shape=(jax.ShapeDtypeStruct((SHARD, D),...]
    div x1 -> x0, other arithmetic: 1.73 us -> none  [per_device(): update_fc2 = (sums[1].T + noise_weight * noise_fc2) / SELECTED]
    slice x1 -> x0, local copies, waits for them, and re-layouts: 1.19 us -> none  [per_device(): total[0, 0] / SELECTED]
    pallas_call x1, Pallas kernels: 28.7 us -> 27.5 us  [per_device(): pl.pallas_call(gather_kernel, out_shape=(jax.ShapeDtypeStruct((2, NY, NX,...]
where the time goes in v2:
time: 91.6 us; the launch traced here: 91.3 us
  Pallas kernels  90 us (98%)
  between operations  1.29 us (1%)
    pallas_call x1, Pallas kernels, per_device(): pl.pallas_call(reduce_kernel, out_shape=(jax.ShapeDtypeStruct((2, SHARD,...  54.1 us
    pallas_call x1, Pallas kernels, per_device(): pl.pallas_call(gather_kernel, out_shape=(jax.ShapeDtypeStruct((2, NY, NX,...  27.5 us
    pallas_call x1, Pallas kernels, per_device(): pl.pallas_call(compute_kernel, out_shape=(jax.ShapeDtypeStruct((2, FF, D)...  3.99 us
    pallas_call x1, Pallas kernels, per_device(): pl.pallas_call(conv_kernel, out_shape=jax.ShapeDtypeStruct((NDP, 8, 128),...  2.54 us

profile of v2, /device:TPU:1, one launch (start us, length us, event | category | flops | bytes accessed | tf_op | source)
XLA Modules:
  0.0 91.3 jit_solution(3177872998094691189)
XLA Ops:
  1.3 2.5 %conv.1.msg_ref = f32[16,8,128]{2,1,0:T(8,128)} custom-call(bf16[1024,512]{1,0:T(8,128)(2,1)} %bitcast.28, bf16[72,512]{1,0:T(8,128)(2,1)} %bitcast.31), custom_call_target="tpu_custom_call" | custom-call | tf_op jit(solution)/shard_map/conv/pallas_call | solution.py:705
  3.8 27.5 %gather.1 = (bf16[2,4,4,2,48,384]{5,4,3,2,1,0:T(8,128)(2,1)}, f32[16,8,128]{2,1,0:T(8,128)}) custom-call(bf16[96,384]{1,0:T(8,128)(2,1)} %bitcast.32, bf16[96,384]{1,0:T(8,128)(2,1)} %bitcast.33, f32[16,8,128]{2,1,0:T(8,128)} %conv.1.msg_ref), custom_call_target="tpu_custom_call" | custom-call | tf_op jit(solution)/shard_map/gather/pallas_call | solution.py:712
  31.4 4.0 %example.1 = (bf16[2,1536,384]{2,1,0:T(8,128)(2,1)}, f32[8,128]{1,0:T(8,128)}, f32[64,128]{1,0:T(8,128)}) custom-call(s32[1,4]{1,0:T(1,128)} %bitcast.38, s32[2,4]{1,0:T(2,128)} %bitcast.37, s32[1,4]{1,0:T(1,128)} %bitcast.39, s32[1,1]{1,0:T(1,128)S(6)} %copy.24.selected_ref, f32[2,1000]{1,0:T(2,128)} %constant.6.clone.table_ref, ...), custom_call_target="tpu_custom_call" | custom-call | tf_op jit(solution)/shard_map/example/pallas_call | solution.py:729
  35.3 54.1 %reduce.1 = (f32[2,96,384]{2,1,0:T(8,128)}, f32[8,128]{1,0:T(8,128)}) custom-call(bf16[2,4,4,2,48,384]{5,4,3,2,1,0:T(8,128)(2,1)} %bitcast.26, f32[8,128]{1,0:T(8,128)} %get-tuple-element.17.loss_ref), custom_call_target="tpu_custom_call" | custom-call | tf_op jit(solution)/shard_map/reduce/pallas_call | solution.py:775
  89.5 1.8 %finish.1 = (f32[96,384]{1,0:T(8,128)}, f32[96,384]{1,0:T(8,128)}, f32[1,1]{1,0:T(1,128)}) custom-call(f32[2,96,384]{2,1,0:T(8,128)} %get-tuple-element.18.sum_ref, f32[8,128]{1,0:T(8,128)} %get-tuple-element.19.total_ref, f32[96,384]{1,0:T(8,128)} %bitcast.29, f32[96,384]{1,0:T(8,128)} %bitcast.30), custom_call_target="tpu_custom_call" | custom-call | tf_op jit(solution)/shard_map/finish/pallas_call | solution.py:803

commit v3 on v1

v3 whole, which is shorter than its diff:
```python
import math

import jax
import jax.numpy as jnp
import ml_dtypes
import numpy as np
from jax import lax
from jax.experimental import pallas as pl
from jax.experimental.pallas import tpu as pltpu
from jax.sharding import Mesh
from jax.sharding import PartitionSpec as P

MESH = pl.DeviceIdType.MESH
DP = ("dp_0", "dp_1")
FSDP = ("fsdp_0", "fsdp_1")
NZ, NC, NY, NX = 8, 2, 4, 4
NDP = NZ * NC
D, FF, TOK, FCH = 384, 1536, 1024, 512
SHARD = FF // (NY * NX)
HALF = SHARD // 2
SIDE, LC, AUG, TSTEPS = 32, 4, 4, 1000
SELECTED = 128
CHUNK = 384
PIECE = 5
TILES = NZ * PIECE
USED_TILES = (SHARD // 8) * (D // 128)
clip_offset = 1e-05
noise_weight = 16.0
norm_epsilon = 1e-06
VMEM_SPEC = pl.BlockSpec(memory_space=pltpu.VMEM)
ANY_SPEC = pl.BlockSpec(memory_space=pl.ANY)
SMEM_SPEC = pl.BlockSpec(memory_space=pltpu.SMEM)
F32, BF16 = jnp.float32, jnp.bfloat16


def three_parts(table):
    high = table.astype(np.float32).astype(ml_dtypes.bfloat16)
    rest = table.astype(np.float32) - high.astype(np.float32)
    middle = rest.astype(ml_dtypes.bfloat16)
    low = (rest - middle.astype(np.float32)).astype(ml_dtypes.bfloat16)
    return high, middle, low


def position_rows():
    side, quarter = SIDE // 2, D // 4
    frequency = 1.0 / 10000.0 ** (np.arange(quarter) / quarter)
    angles = np.arange(side)[:, None] * frequency[None, :]
    line = np.concatenate([np.sin(angles), np.cos(angles)], axis=1)
    parts = three_parts(line)
    zero = np.zeros_like(parts[0])
    rows = [np.concatenate([p, zero], axis=1) for p in parts]
    cols = [np.concatenate([zero, p], axis=1) for p in parts]
    return np.concatenate(rows + cols, axis=0)


def blend_tables():
    beta = 0.0001 + np.arange(TSTEPS) * (0.02 - 0.0001) / (TSTEPS - 1)
    alpha_bar = np.cumprod(1.0 - beta)
    return np.stack([np.sqrt(alpha_bar), np.sqrt(1.0 - alpha_bar)]).astype(np.float32)


def time_rates():
    steps = np.arange(128, dtype=np.float32)
    scaled = np.float32(-math.log(10000.0)) * steps / np.float32(128)
    return np.exp(scaled).astype(np.float32).reshape(1, 128)


def place():
    return tuple(lax.axis_index(a) for a in ("dp_0", "dp_1", "fsdp_0", "fsdp_1"))


def split_three(value):
    high = value.astype(BF16)
    rest = value - high.astype(F32)
    middle = rest.astype(BF16)
    low = (rest - middle.astype(F32)).astype(BF16)
    return jnp.concatenate([high, middle, low], axis=0)


def joined_three(value, rows):
    return (value[2 * rows :] + value[rows : 2 * rows]) + value[:rows]


def step_kernel(
    flips_ref,
    crops_ref,
    steps_ref,
    selected_ref,
    table_ref,
    x_ref,
    taps_ref,
    w1_ref,
    w2s_ref,
    vae_ref,
    noise_ref,
    wp_ref,
    pos_ref,
    rates_ref,
    wt_ref,
    wa_ref,
    wf_ref,
    sum_ref,
    total_ref,
    moments_ref,
    *scratch,
):
    (x_buf, wt_buf, wa_buf, all_ref, msg_ref, got_ref) = scratch[:6]
    (rows_ref, pads_ref, shift_ref, scale_ref, gate_ref, tok_ref, modt_ref) = scratch[6:13]
    (mod_ref, w2_ref, hid_ref, slope_ref, target_ref, gbt_ref, gb_ref) = scratch[13:20]
    (square_ref, own_ref, keep_ref, send_ref, r0, s1, r1, acc, r2) = scratch[20:29]
    (tiles, r3, whole, l1, l2) = scratch[29:34]
    (g1_send, g1_recv, g2_send, g2_recv, p_send, p_recv) = scratch[34:40]
    (s1_send, s1_recv, s2_send, s2_recv) = scratch[40:44]
    (m_send, m_recv, q_send, q_recv, z_send, z_recv) = scratch[44:50]
    (a_send, a_recv, f_send, f_recv, l_send, l_recv, c_sem) = scratch[50:]
    z, c, y, x = place()
    me = z * NC + c
    partner = {"dp_1": 1 - c}
    lane = lax.broadcasted_iota(jnp.int32, (8, 128), 1)
    zero = jnp.zeros((8, 128), F32)

    def x_at(k):
        return lax.rem(x + k, NX)

    def y_at(k):
        return lax.rem(y + k, NY)

    def z_at(k):
        return lax.rem(z + k, NZ)

    def dp_at(k):
        return lax.rem(me + k, NDP)

    def dp_device(k):
        other = dp_at(k)
        return {"dp_0": other // NC, "dp_1": lax.rem(other, NC)}

    def remote(src, dst, send, recv, device):
        return pltpu.make_async_remote_copy(
            src_ref=src,
            dst_ref=dst,
            send_sem=send,
            recv_sem=recv,
            device_id=device,
            device_id_type=MESH,
        )

    def first_to(half, k):
        return {"fsdp_1": x_at(k)} if half == 0 else {"fsdp_0": y_at(k)}

    def second_to(half, k):
        return {"fsdp_0": y_at(k)} if half == 0 else {"fsdp_1": x_at(k)}

    def second_at(half, k):
        return y_at(k) if half == 0 else x_at(k)

    barrier = pltpu.get_barrier_semaphore()
    for k in range(1, NX):
        pl.semaphore_signal(barrier, 1, device_id={"fsdp_1": x_at(k)}, device_id_type=MESH)
        pl.semaphore_signal(barrier, 1, device_id={"fsdp_0": y_at(k)}, device_id_type=MESH)
    for k in range(1, NDP):
        pl.semaphore_signal(barrier, 1, device_id=dp_device(k), device_id_type=MESH)
    x_copy = pltpu.make_async_copy(x_ref, x_buf, c_sem.at[0])
    wt_copy = pltpu.make_async_copy(wt_ref, wt_buf, c_sem.at[1])
    wa_copy = pltpu.make_async_copy(wa_ref, wa_buf, c_sem.at[2])
    x_copy.start()
    wt_copy.start()
    wa_copy.start()
    own_shard = jnp.where(c == 0, w1_ref[...], w2s_ref[...])
    all_ref[c, y, x, 0] = own_shard[:HALF]
    all_ref[c, y, x, 1] = own_shard[HALF:]
    pl.semaphore_wait(barrier, NX - 1 + NY - 1 + NDP - 1)

    def message(k):
        return remote(
            msg_ref.at[dp_at(k)], got_ref.at[me], m_send.at[k], m_recv.at[k], dp_device(k)
        )

    def gather_first(half, k):
        at = all_ref.at[c, y, x, half]
        return remote(at, at, g1_send.at[half, k], g1_recv.at[half, k], first_to(half, k))

    def line(half, k):
        if half == 0:
            return all_ref.at[c, y_at(NY - k), :, 0]
        return all_ref.at[c, :, x_at(NX - k), 1]

    def gather_second(half, k):
        at = line(half, 0)
        return remote(at, at, g2_send.at[half, k], g2_recv.at[half, k], second_to(half, k))

    def across(half, k):
        at = line(half, k)
        return remote(at, at, p_send.at[half, k], p_recv.at[half, k], partner)

    messages = [message(k) for k in range(1, NDP)]
    early = {(h, k): gather_first(h, k) for k in (1, 3, 2) for h in range(2)}
    late = {(h, k): gather_second(h, k) for k in (1, 3, 2) for h in range(2)}
    crossed = {(h, k): across(h, k) for k in (0, 1, 3, 2) for h in range(2)}
    for copy in early.values():
        copy.start()
    x_copy.wait()
    taps = lax.dot_general(
        taps_ref[...], x_buf[...], (((1,), (1,)), ((), ())), preferred_element_type=F32
    )
    col = lane % SIDE

    def tap(dy, dx, v):
        at = (dy * 3 + dx) * 8
        return taps[at : at + 8, 128 * v : 128 * v + 128]

    for v in range(8):
        rows = []
        for dy in range(3):
            left = jnp.where(col == 0, zero, pltpu.roll(tap(dy, 0, v), 1, 1))
            right = jnp.where(col == SIDE - 1, zero, pltpu.roll(tap(dy, 2, v), 127, 1))
            rows.append(left + tap(dy, 1, v) + right)
        for odd in range(2):
            parts = [pltpu.roll(r, 64, 1) if odd else r for r in rows]
            parts = [jnp.where(lane < 64, r, zero) for r in parts]
            msg_ref[2 * v + odd] = (
                parts[2] + pltpu.roll(parts[1], 32, 1) + pltpu.roll(parts[0], 64, 1)
            )
    got_ref[me] = msg_ref[me]
    for m in messages:
        m.start()
    for copy in early.values():
        copy.wait_recv()
    for copy in late.values():
        copy.start()
    for h in range(2):
        crossed[h, 0].start()
    wt_copy.wait()
    wa_copy.wait()

    row = lax.broadcasted_iota(jnp.int32, (8, 128), 0)
    steps = jnp.zeros((8, 128), F32)
    for a in range(AUG):
        steps = jnp.where(row == a, steps_ref[0, a].astype(F32), steps)
    phases = steps * rates_ref[...]
    stamp = jnp.concatenate([jnp.cos(phases), jnp.sin(phases)], axis=1).astype(BF16)
    raw = jnp.dot(stamp, wt_buf[...], preferred_element_type=F32)
    conditioning = (raw * (1.0 / (1.0 + jnp.exp(-raw)))).astype(BF16)
    modulation = jnp.dot(conditioning, wa_buf[...], preferred_element_type=F32)
    views = [jnp.broadcast_to(modulation[a : a + 1], (16, 3 * D)) for a in range(AUG)]
    turned = jnp.concatenate(views + views, axis=0).T
    shift_ref[...] = turned[:D]
    scale_ref[...] = 1.0 + turned[D : 2 * D]
    gate_ref[...] = turned[2 * D :]

    for m in messages:
        m.wait_recv()
    for k in range(8):
        low = pltpu.roll(got_ref[2 * k], 96, 1)
        above = pltpu.roll(got_ref[2 * k + 2], 96, 1) if k < 7 else zero
        high = pltpu.roll(got_ref[2 * k + 1], 32, 1)
        below = pltpu.roll(got_ref[2 * k - 1], 32, 1) if k > 0 else zero
        four = jnp.where(lane < 96, low, above) + jnp.where(lane >= 32, high, below)
        for r in range(4):
            at = (4 * k + r) * 8
            rows_ref[at : at + 8, :] = pltpu.roll(four, 128 - 32 * r, 1) if r else four
    wide = lax.broadcasted_iota(jnp.int32, (SIDE, 128), 1) // SIDE
    halves = []
    for h in range(2):
        value = rows_ref[pl.ds(4 * h, SIDE, stride=8), :]
        for ch in range(1, 4):
            part = rows_ref[pl.ds(4 * h + ch, SIDE, stride=8), :]
            value = jnp.where(wide == ch, pltpu.roll(part, 32 * ch, 1), value)
        halves.append(value)
    by_channel = jnp.concatenate(halves, axis=1)
    source = lax.broadcasted_iota(jnp.int32, (256, 512), 0)
    goal = lax.broadcasted_iota(jnp.int32, (256, 512), 1)
    channel, column = source // SIDE, source % SIDE
    natural = column * 8 + channel
    apart = 256 + (channel // 4) * 128 + column * 4 + channel % 4
    spread = jnp.where((goal == natural) | (goal == apart), 1.0, 0.0).astype(BF16)
    placed = joined_three(
        jnp.dot(split_three(by_channel), spread, preferred_element_type=F32), SIDE
    )
    moments_ref[pl.ds(0, SIDE, stride=2), :] = placed[:, 0:128]
    moments_ref[pl.ds(1, SIDE, stride=2), :] = placed[:, 128:256]

    latent = placed[:, 256:384] + jnp.exp(0.5 * placed[:, 384:512]) * vae_ref[...]
    source = lax.broadcasted_iota(jnp.int32, (128, 128), 0)
    goal = lax.broadcasted_iota(jnp.int32, (128, 128), 1)
    maps = []
    for a in range(AUG):
        cell = goal // LC + crops_ref[1, a] - 2
        inside = (cell >= 0) & (cell < SIDE)
        mirror = (flips_ref[0, a] == 1).astype(jnp.int32)
        cell = cell + mirror * (SIDE - 1 - 2 * cell)
        match = inside & (source == cell * LC + goal % LC)
        maps.append(jnp.where(match, 1.0, 0.0).astype(BF16))
    columns = jnp.dot(
        split_three(latent), jnp.concatenate(maps, axis=1), preferred_element_type=F32
    )
    columns = joined_three(columns, SIDE)
    noised, noises = [], []
    for a in range(AUG):
        pads_ref[a] = jnp.zeros((40, 128), F32)
        pads_ref[a, 2 : 2 + SIDE, :] = columns[:, 128 * a : 128 * a + 128]
    for dr in range(2):
        for a in range(AUG):
            view = pads_ref[a, pl.ds(crops_ref[0, a] + dr, 16, stride=2), :]
            noise = noise_ref[pl.ds(dr * 4 + a, 16, stride=8), :]
            step = steps_ref[0, a]
            noised.append(table_ref[0, step] * view + table_ref[1, step] * noise)
            noises.append(noise)

    def patched(pieces):
        turned = jnp.concatenate(pieces, axis=0).T
        first, last = [], []
        for m in range(8):
            even = turned[16 * m : 16 * m + 8]
            odd = turned[16 * m + 8 : 16 * m + 16]
            first.append(jnp.where(lane < 64, even, pltpu.roll(odd, 64, 1)))
            last.append(jnp.where(lane < 64, pltpu.roll(even, 64, 1), odd))
        return jnp.concatenate(
            [jnp.concatenate(first, axis=1), jnp.concatenate(last, axis=1)], axis=0
        )

    patches = patched(noised).astype(BF16)
    target_ref[...] = patched(noises)

    which = lax.broadcasted_iota(jnp.int32, (96, TOK), 0)
    token = lax.broadcasted_iota(jnp.int32, (96, TOK), 1)
    cell = jnp.where(which < 48, token % 16, token // 64)
    marks = jnp.where(which % 16 == cell, 1.0, 0.0).astype(BF16)
    tok_ref[...] = lax.dot_general(
        jnp.concatenate([wp_ref[...], pos_ref[...]], axis=0),
        jnp.concatenate([patches, marks], axis=0),
        (((0,), (0,)), ((), ())),
        preferred_element_type=F32,
    )

    for k in (1, 3):
        for h in range(2):
            late[h, k].wait_recv()
            crossed[h, k].start()

    @pl.loop(0, TOK // 128)
    def _(m):
        at = pl.ds(pl.multiple_of(m * 128, 128), 128)
        value = tok_ref[:, at]
        center = value - jnp.sum(value, axis=0, keepdims=True) * (1.0 / D)
        variance = jnp.sum(center * center, axis=0, keepdims=True) * (1.0 / D)
        normed = center * lax.rsqrt(variance + norm_epsilon)
        out = normed * scale_ref[...] + shift_ref[...]
        modt_ref[:, at] = out.astype(BF16)
        mod_ref[at, :] = out.T.astype(BF16)

    for k in (2,):
        for h in range(2):
            late[h, k].wait_recv()
            crossed[h, k].start()

    for copy in crossed.values():
        copy.wait_recv()
    flat_weights = all_ref.reshape(2, FF, D)

    def weights(w, at):
        return flat_weights[w, at, :]

    @pl.loop(0, FF // 128)
    def _(m):
        at = pl.ds(pl.multiple_of(m * 128, 128), 128)
        w2_ref[:, at] = weights(1, at).astype(F32).T.astype(BF16)

    root = math.sqrt(2.0 / math.pi)

    @pl.loop(0, FF // CHUNK)
    def _(f):
        at = pl.ds(pl.multiple_of(f * CHUNK, CHUNK), CHUNK)
        pre = jnp.dot(weights(0, at), modt_ref[...], preferred_element_type=F32)
        squared = pre * pre
        inner = pre * (squared * (root * 0.044715) + root)
        share = 0.5 * jnp.tanh(inner) + 0.5
        hidden = pre * share
        hid_ref[at, :] = hidden.astype(BF16)
        slope = (1.0 - share) * hidden * (squared * (6.0 * root * 0.044715) + 2.0 * root)
        slope_ref[at, :] = slope + share

    own_ref[1] = jnp.zeros((8, 128), F32)

    @pl.loop(0, TOK // 256)
    def _(m):
        at = pl.ds(pl.multiple_of(m * 256, 256), 256)
        branch = jnp.dot(w2_ref[...], hid_ref[:, at], preferred_element_type=F32)
        gate = jnp.concatenate([gate_ref[...], gate_ref[...]], axis=1)
        mixed = tok_ref[:, at] + gate * branch
        center = mixed - jnp.sum(mixed, axis=0, keepdims=True) * (1.0 / D)
        variance = jnp.sum(center * center, axis=0, keepdims=True) * (1.0 / D)
        inverse = lax.rsqrt(variance + norm_epsilon)
        normed = center * inverse
        predicted = jnp.dot(wf_ref[...], normed.astype(BF16), preferred_element_type=F32)
        residue = predicted - target_ref[:, at]
        own_ref[1] += jnp.sum(residue * residue) * (1.0 / (TOK * 16))
        grad_pred = (residue * (2.0 / (TOK * 16))).astype(BF16)
        grad_normed = lax.dot_general(
            wf_ref[...], grad_pred, (((0,), (0,)), ((), ())), preferred_element_type=F32
        )
        mean = jnp.sum(grad_normed, axis=0, keepdims=True) * (1.0 / D)
        along = jnp.sum(grad_normed * normed, axis=0, keepdims=True) * (1.0 / D)
        grad_mixed = inverse * (grad_normed - mean - normed * along)
        grad_branch = gate * grad_mixed
        gbt_ref[:, at] = grad_branch.astype(BF16)
        gb_ref[at, :] = grad_branch.T.astype(BF16)

    square_ref[...] = jnp.zeros_like(square_ref)
    chosen = selected_ref[0, 0] == 1

    def swap(f):
        return remote(send_ref.at[f], r0.at[f], q_send.at[f], q_recv.at[f], partner)

    @pl.loop(0, NY)
    def _(f):
        at = pl.ds(pl.multiple_of(f * CHUNK, CHUNK), CHUNK)
        grad_hidden = jnp.dot(weights(1, at), gbt_ref[...], preferred_element_type=F32)
        grad_pre = (slope_ref[at, :] * grad_hidden).astype(BF16)
        grad_1 = jnp.dot(grad_pre, mod_ref[...], preferred_element_type=F32)
        grad_2 = jnp.dot(hid_ref[at, :], gb_ref[...], preferred_element_type=F32)
        grad_1 = jnp.where(chosen, grad_1, 0.0)
        grad_2 = jnp.where(chosen, grad_2, 0.0)
        kept = jnp.where(c == 0, grad_1, grad_2)
        sent = jnp.where(c == 0, grad_2, grad_1)
        keep_ref[f] = kept.reshape(NX, 2, HALF, D)
        send_ref[f] = sent.astype(BF16).reshape(NX, 2, HALF, D)
        swap(f).start()
        square_ref[...] += jnp.sum(
            grad_1 * grad_1 + grad_2 * grad_2, axis=0, keepdims=True
        )

    total = jnp.sum(square_ref[...], axis=1, keepdims=True)
    factor = 1.0 / (jnp.sqrt(total * (1.0 / (2 * D * FF))) + clip_offset)
    own_ref[0] = jnp.broadcast_to(factor, (8, 128))
    own_ref[1] = jnp.where(chosen, own_ref[1], 0.0)
    loss_0 = remote(own_ref.at[pl.ds(0, 2)], own_ref.at[pl.ds(2, 2)], l_send.at[0], l_recv.at[0], partner)
    loss_0.start()
    for f in range(NY):
        swap(f).wait_recv()
    loss_0.wait_recv()
    mine = own_ref[0, 0:1, 0:1]
    other = own_ref[2, 0:1, 0:1]

    def part(half, k, j):
        if half == 0:
            return (j, x_at(k), 0)
        return (y_at(k), j, 1)

    def chip(half, k, j):
        at = part(half, k, j)
        return keep_ref[at] * mine + r0[at].astype(F32) * other

    firsts = {}
    for k in (2, 1, 3, 0):
        for h in range(2):
            for j in range(4):
                value = chip(h, k, j)
                if k == 0:
                    acc[h, j] = value
                else:
                    s1[h, k - 1, j] = value.astype(BF16)
            if k > 0:
                firsts[h, k] = remote(
                    s1.at[h, k - 1],
                    r1.at[h, k - 1],
                    s1_send.at[h, k],
                    s1_recv.at[h, k],
                    first_to(h, k),
                )
                firsts[h, k].start()
    l1[x] = own_ref[1] + own_ref[3]
    losses = [loss_0]
    for k in range(1, NX):
        copy = remote(l1.at[x], l1.at[x], l_send.at[k], l_recv.at[k], {"fsdp_1": x_at(k)})
        copy.start()
        losses.append(copy)
    seconds = {}
    for h in range(2):
        for k in (1, 3, 2):
            firsts[h, k].wait_recv()
        for k in (2, 1, 3, 0):
            j = second_at(h, k)
            acc[h, j] = (acc[h, j] + r1[h, 0, j].astype(F32)) + (
                r1[h, 1, j].astype(F32) + r1[h, 2, j].astype(F32)
            )
            if k > 0:
                seconds[h, k] = remote(
                    acc.at[h, j],
                    r2.at[h, k - 1],
                    s2_send.at[h, k],
                    s2_recv.at[h, k],
                    second_to(h, k),
                )
                seconds[h, k].start()
    for copy in losses[1:]:
        copy.wait_recv()
    l2[y] = (l1[0] + l1[1]) + (l1[2] + l1[3])
    for k in range(1, NY):
        copy = remote(
            l2.at[y], l2.at[y], l_send.at[3 + k], l_recv.at[3 + k], {"fsdp_0": y_at(k)}
        )
        copy.start()
        losses.append(copy)
    for h in range(2):
        for k in (1, 3, 2):
            seconds[h, k].wait_recv()
        j = second_at(h, 0)
        value = (acc[h, j] + r2[h, 0]) + (r2[h, 1] + r2[h, 2])
        for i in range(HALF // 8):
            for n in range(D // 128):
                t = (h * (HALF // 8) + i) * (D // 128) + n
                tiles[t // PIECE, t % PIECE] = value[8 * i : 8 * i + 8, 128 * n : 128 * n + 128]
    for copy in losses[4:]:
        copy.wait_recv()
    at = USED_TILES
    tiles[at // PIECE, at % PIECE] = (l2[0] + l2[1]) + (l2[2] + l2[3])
    for t in range(USED_TILES + 1, TILES):
        tiles[t // PIECE, t % PIECE] = jnp.zeros((8, 128), F32)

    order = (4, 3, 5, 2, 6, 1, 7)
    thirds = []
    for k in order:
        copy = remote(
            tiles.at[z_at(k)], r3.at[z], z_send.at[k], z_recv.at[k], {"dp_0": z_at(k)}
        )
        copy.start()
        thirds.append(copy)
    r3[z] = tiles[z]
    for copy in thirds:
        copy.wait_recv()
    value = r3[0]
    for k in range(1, NZ):
        value = value + r3[k]
    whole[c, z] = value
    spreads = {}
    for k in order:
        spreads[k] = remote(
            whole.at[c, z], whole.at[c, z], a_send.at[k], a_recv.at[k], {"dp_0": z_at(k)}
        )
        spreads[k].start()
    crossings = []
    for k in (0, 7, 1, 6, 2, 5, 3, 4):
        if k > 0:
            spreads[k].wait_recv()
        at = z_at(NZ - k) if k > 0 else z
        copy = remote(whole.at[c, at], whole.at[c, at], f_send.at[k], f_recv.at[k], partner)
        copy.start()
        crossings.append(copy)
    for copy in crossings:
        copy.wait_recv()
    for w in range(2):
        for t in range(USED_TILES):
            i, n = t // (D // 128), t % (D // 128)
            sum_ref[w, 8 * i : 8 * i + 8, 128 * n : 128 * n + 128] = whole[
                w, t // PIECE, t % PIECE
            ]
    total_ref[...] = whole[0, USED_TILES // PIECE, USED_TILES % PIECE]
    for f in range(NY):
        swap(f).wait_send()
    for group in (early, late, crossed, firsts, seconds, spreads):
        for copy in group.values():
            copy.wait_send()
    for group in (messages, losses, thirds, crossings):
        for copy in group:
            copy.wait_send()


def finish_kernel(sum_ref, total_ref, moved_ref, n1_ref, n2_ref, *outs):
    u1_ref, u2_ref, mean_ref, moments_ref = outs
    u1_ref[...] = (sum_ref[0] + noise_weight * n1_ref[...]) * (1.0 / SELECTED)
    u2_ref[...] = (sum_ref[1] + noise_weight * n2_ref[...]) * (1.0 / SELECTED)
    mean_ref[...] = total_ref[0:1, 0:1] * (1.0 / SELECTED)
    moments_ref[...] = moved_ref[...]


def per_device(
    features,
    conv_weight,
    vae_noise,
    flips,
    crops,
    tsteps,
    diffusion_noise,
    selected,
    w_patch,
    w_time,
    w_ada,
    w_fc1,
    w_fc2,
    w_final,
    noise_fc1,
    noise_fc2,
):
    dma = pltpu.SemaphoreType.DMA
    pixels = features.reshape(TOK, FCH)
    taps = conv_weight.transpose(0, 1, 3, 2).reshape(72, FCH)
    views = diffusion_noise.reshape(AUG, SIDE, SIDE * LC).transpose(1, 0, 2)
    grid = (NY, NX, 2, HALF, D)
    tile = (8, 128)
    vmem = pltpu.VMEM
    sums, total, moved = pl.pallas_call(
        step_kernel,
        out_shape=(
            jax.ShapeDtypeStruct((2, SHARD, D), F32),
            jax.ShapeDtypeStruct(tile, F32),
            jax.ShapeDtypeStruct((2 * SIDE, 128), F32),
        ),
        in_specs=[SMEM_SPEC] * 5
        + [ANY_SPEC]
        + [VMEM_SPEC] * 8
        + [ANY_SPEC] * 2
        + [VMEM_SPEC],
        out_specs=(VMEM_SPEC,) * 3,
        scratch_shapes=[
            vmem((TOK, FCH), BF16),
            vmem((256, D), BF16),
            vmem((D, 3 * D), BF16),
            vmem((2,) + grid, BF16),
            vmem((NDP,) + tile, F32),
            vmem((NDP,) + tile, F32),
            vmem((256, 128), F32),
            vmem((AUG, 40, 128), F32),
            vmem((D, 128), F32),
            vmem((D, 128), F32),
            vmem((D, 128), F32),
            vmem((D, TOK), F32),
            vmem((D, TOK), BF16),
            vmem((TOK, D), BF16),
            vmem((D, FF), BF16),
            vmem((FF, TOK), BF16),
            vmem((FF, TOK), F32),
            vmem((16, TOK), F32),
            vmem((D, TOK), BF16),
            vmem((TOK, D), BF16),
            vmem((1, D), F32),
            vmem((4,) + tile, F32),
            vmem(grid, F32),
            vmem(grid, BF16),
            vmem(grid, BF16),
            vmem((2, 3, 4, HALF, D), BF16),
            vmem((2, 3, 4, HALF, D), BF16),
            vmem((2, 4, HALF, D), F32),
            vmem((2, 3, HALF, D), F32),
            vmem((NZ, PIECE) + tile, F32),
            vmem((NZ, PIECE) + tile, F32),
            vmem((2, NZ, PIECE) + tile, F32),
            vmem((NX,) + tile, F32),
            vmem((NY,) + tile, F32),
        ]
        + [dma((2, 4))] * 10
        + [dma((NDP,))] * 2
        + [dma((NZ,))] * 10
        + [dma((3,))],
        compiler_params=pltpu.CompilerParams(
            collective_id=0, has_side_effects=True, vmem_limit_bytes=56 << 20
        ),
        name="step",
    )(
        flips.reshape(1, AUG),
        crops.reshape(AUG, 2).T,
        tsteps.reshape(1, AUG),
        selected,
        jnp.asarray(blend_tables()),
        pixels,
        taps,
        w_fc1.T,
        w_fc2.T,
        vae_noise.reshape(SIDE, SIDE * LC),
        views.reshape(SIDE * AUG, SIDE * LC),
        w_patch,
        jnp.asarray(position_rows()),
        jnp.asarray(time_rates()),
        w_time,
        w_ada,
        w_final.T,
    )
    update_1, update_2, mean_loss, moments = pl.pallas_call(
        finish_kernel,
        out_shape=(
            jax.ShapeDtypeStruct((SHARD, D), F32),
            jax.ShapeDtypeStruct((SHARD, D), F32),
            jax.ShapeDtypeStruct((1, 1), F32),
            jax.ShapeDtypeStruct((2 * SIDE, 128), F32),
        ),
        in_specs=[VMEM_SPEC] * 5,
        out_specs=(VMEM_SPEC,) * 4,
        name="finish",
    )(sums, total, moved, noise_fc1.T, noise_fc2.T)
    return (update_1.T, update_2.T, mean_loss.reshape(()), moments.reshape(1, 1, -1))


def solution(mesh):
    split = Mesh(mesh.devices.reshape(NZ, NC, NY, NX), DP + FSDP)
    return jax.shard_map(
        per_device,
        mesh=split,
        in_specs=(
            P(FSDP, None, DP, None, None),
            P(),
            P(DP, FSDP, None),
            P(DP, FSDP, None),
            P(DP, FSDP, None, None),
            P(DP, FSDP, None),
            P(DP, FSDP, None, None),
            P(DP, FSDP),
            P(),
            P(),
            P(),
            P(None, FSDP),
            P(None, FSDP),
            P(),
            P(None, FSDP),
            P(None, FSDP),
        ),
        out_specs=(P(None, FSDP), P(None, FSDP), P(), P(DP, FSDP, None)),
        check_vma=False,
    )
```

time: 95.1 us -> 76 us (0.80)
  Pallas kernels: 88.8 us -> 74.5 us
  between operations: 3.11 us -> 1.29 us
  other arithmetic: 1.73 us -> 0 us
  local copies, waits for them, and re-layouts: 1.2 us -> 0 us
    pallas_call x4 -> x2, Pallas kernels: 88.8 us -> 74.5 us  [the longest x1 72.7 us: per_device(): pl.pallas_call(step_kernel, out_shape=(jax.ShapeDtypeStruct((2, SHARD, D)...]
    div x1 -> x0, other arithmetic: 1.73 us -> none  [per_device(): update_fc2 = (sums[1].T + noise_weight * noise_fc2) / SELECTED]
    slice x1 -> x0, local copies, waits for them, and re-layouts: 1.19 us -> none  [per_device(): total[0, 0] / SELECTED]
where the time goes in v3:
time: 76 us; the launch traced here: 75.8 us
  Pallas kernels  74.5 us (98%)
  between operations  1.29 us (2%)
    pallas_call x1, Pallas kernels, per_device(): pl.pallas_call(step_kernel, out_shape=(jax.ShapeDtypeStruct((2, SHARD, D)...  72.7 us
    pallas_call x1, Pallas kernels, per_device(): pl.pallas_call(finish_kernel, out_shape=(jax.ShapeDtypeStruct((SHARD, D),...  1.85 us

profile of v3, /device:TPU:1, one launch (start us, length us, event | category | flops | bytes accessed | tf_op | source)
XLA Modules:
  0.0 75.8 jit_solution(13313928891808316720)
XLA Ops:
  1.3 72.7 %step.1 = (f32[2,96,384]{2,1,0:T(8,128)}, f32[8,128]{1,0:T(8,128)}, f32[64,128]{1,0:T(8,128)}) custom-call(s32[1,4]{1,0:T(1,128)} %bitcast.34, s32[2,4]{1,0:T(2,128)} %bitcast.33, s32[1,4]{1,0:T(1,128)} %bitcast.35, s32[1,1]{1,0:T(1,128)S(6)} %copy.24.selected_ref, f32[2,1000]{1,0:T(2,128)} %constant.6.clone.table_ref, bf16[1024,512]{1,0:T(8,128)(2,1)} %bitcast.24, ...), custom_call_target="tpu_custom_call" | custom-call | tf_op jit(solution)/shard_map/step/pallas_call | solution.py:602
  74.0 1.9 %finish.1 = (f32[96,384]{1,0:T(8,128)}, f32[96,384]{1,0:T(8,128)}, f32[1,1]{1,0:T(1,128)}, f32[64,128]{1,0:T(8,128)}) custom-call(f32[2,96,384]{2,1,0:T(8,128)} %get-tuple-element.11.sum_ref, f32[8,128]{1,0:T(8,128)} %get-tuple-element.12.total_ref, f32[64,128]{1,0:T(8,128)} %get-tuple-element.13.moved_ref, f32[96,384]{1,0:T(8,128)} %bitcast.25, ...), custom_call_target="tpu_custom_call" | custom-call | tf_op jit(solution)/shard_map/finish/pallas_call | solution.py:678

commit v4 on v3

--- a/solution.py
+++ b/solution.py
@@ -21,6 +21,7 @@
 SIDE, LC, AUG, TSTEPS = 32, 4, 4, 1000
 SELECTED = 128
 CHUNK = 384
+WIDE = 512
 PIECE = 5
 TILES = NZ * PIECE
 USED_TILES = (SHARD // 8) * (D // 128)
@@ -69,6 +70,10 @@
     return tuple(lax.axis_index(a) for a in ("dp_0", "dp_1", "fsdp_0", "fsdp_1"))
 
 
+def widened(ref):
+    return jnp.concatenate([ref[...]] * (WIDE // 128), axis=1)
+
+
 def split_three(value):
     high = value.astype(BF16)
     rest = value - high.astype(F32)
@@ -81,38 +86,21 @@
     return (value[2 * rows :] + value[rows : 2 * rows]) + value[:rows]
 
 
-def step_kernel(
-    flips_ref,
-    crops_ref,
-    steps_ref,
-    selected_ref,
-    table_ref,
-    x_ref,
-    taps_ref,
-    w1_ref,
-    w2s_ref,
-    vae_ref,
-    noise_ref,
-    wp_ref,
-    pos_ref,
-    rates_ref,
-    wt_ref,
-    wa_ref,
-    wf_ref,
-    sum_ref,
-    total_ref,
-    moments_ref,
-    *scratch,
-):
-    (x_buf, wt_buf, wa_buf, all_ref, msg_ref, got_ref) = scratch[:6]
-    (rows_ref, pads_ref, shift_ref, scale_ref, gate_ref, tok_ref, modt_ref) = scratch[6:13]
-    (mod_ref, w2_ref, hid_ref, slope_ref, target_ref, gbt_ref, gb_ref) = scratch[13:20]
-    (square_ref, own_ref, keep_ref, send_ref, r0, s1, r1, acc, r2) = scratch[20:29]
-    (tiles, r3, whole, l1, l2) = scratch[29:34]
-    (g1_send, g1_recv, g2_send, g2_recv, p_send, p_recv) = scratch[34:40]
-    (s1_send, s1_recv, s2_send, s2_recv) = scratch[40:44]
-    (m_send, m_recv, q_send, q_recv, z_send, z_recv) = scratch[44:50]
-    (a_send, a_recv, f_send, f_recv, l_send, l_recv, c_sem) = scratch[50:]
+def step_kernel(*refs):
+    inputs, (sum_ref, total_ref, moments_ref) = refs[:17], refs[17:20]
+    buffers, scratch = refs[20:37], refs[37:]
+    (flips_ref, crops_ref, steps_ref, selected_ref, table_ref) = buffers[:5]
+    (x_buf, taps_ref, w1_ref, w2s_ref, vae_ref, noise_ref, wp_ref) = buffers[5:12]
+    (pos_ref, rates_ref, wt_buf, wa_buf, wf_ref) = buffers[12:]
+    (all_ref, msg_ref, got_ref) = scratch[:3]
+    (rows_ref, pads_ref, shift_ref, scale_ref, gate_ref, tok_ref, modt_ref) = scratch[3:10]
+    (mod_ref, w2_ref, hid_ref, slope_ref, target_ref, gbt_ref, gb_ref) = scratch[10:17]
+    (square_ref, own_ref, keep_ref, send_ref, r0, s1, r1, acc, c2, r2) = scratch[17:27]
+    (tiles, r3, whole, l0, l1, l2) = scratch[27:33]
+    (g1_send, g1_recv, g2_send, g2_recv, p_send, p_recv) = scratch[33:39]
+    (s2_send, s2_recv, s1_send, s1_recv) = scratch[39:43]
+    (m_send, m_recv, q_send, q_recv, z_send, z_recv) = scratch[43:49]
+    (a_send, a_recv, f_send, f_recv, l_send, l_recv, c_sem) = scratch[49:]
     z, c, y, x = place()
     me = z * NC + c
     partner = {"dp_1": 1 - c}
@@ -160,12 +148,17 @@
         pl.semaphore_signal(barrier, 1, device_id={"fsdp_0": y_at(k)}, device_id_type=MESH)
     for k in range(1, NDP):
         pl.semaphore_signal(barrier, 1, device_id=dp_device(k), device_id_type=MESH)
-    x_copy = pltpu.make_async_copy(x_ref, x_buf, c_sem.at[0])
-    wt_copy = pltpu.make_async_copy(wt_ref, wt_buf, c_sem.at[1])
-    wa_copy = pltpu.make_async_copy(wa_ref, wa_buf, c_sem.at[2])
-    x_copy.start()
-    wt_copy.start()
-    wa_copy.start()
+    loads = [
+        pltpu.make_async_copy(inputs[i], buffers[i], c_sem.at[i]) for i in range(len(inputs))
+    ]
+    shards, pictures = (7, 8), (5, 6)
+    for i in shards + pictures:
+        loads[i].start()
+    for i in range(len(inputs)):
+        if i not in shards + pictures:
+            loads[i].start()
+    for i in shards:
+        loads[i].wait()
     own_shard = jnp.where(c == 0, w1_ref[...], w2s_ref[...])
     all_ref[c, y, x, 0] = own_shard[:HALF]
     all_ref[c, y, x, 1] = own_shard[HALF:]
@@ -199,7 +192,8 @@
     crossed = {(h, k): across(h, k) for k in (0, 1, 3, 2) for h in range(2)}
     for copy in early.values():
         copy.start()
-    x_copy.wait()
+    for i in pictures:
+        loads[i].wait()
     taps = lax.dot_general(
         taps_ref[...], x_buf[...], (((1,), (1,)), ((), ())), preferred_element_type=F32
     )
@@ -230,8 +224,9 @@
         copy.start()
     for h in range(2):
         crossed[h, 0].start()
-    wt_copy.wait()
-    wa_copy.wait()
+    for i in range(len(inputs)):
+        if i not in shards + pictures:
+            loads[i].wait()
 
     row = lax.broadcasted_iota(jnp.int32, (8, 128), 0)
     steps = jnp.zeros((8, 128), F32)
@@ -338,14 +333,14 @@
             late[h, k].wait_recv()
             crossed[h, k].start()
 
-    @pl.loop(0, TOK // 128)
+    @pl.loop(0, TOK // WIDE)
     def _(m):
-        at = pl.ds(pl.multiple_of(m * 128, 128), 128)
+        at = pl.ds(pl.multiple_of(m * WIDE, WIDE), WIDE)
         value = tok_ref[:, at]
         center = value - jnp.sum(value, axis=0, keepdims=True) * (1.0 / D)
         variance = jnp.sum(center * center, axis=0, keepdims=True) * (1.0 / D)
         normed = center * lax.rsqrt(variance + norm_epsilon)
-        out = normed * scale_ref[...] + shift_ref[...]
+        out = normed * widened(scale_ref) + widened(shift_ref)
         modt_ref[:, at] = out.astype(BF16)
         mod_ref[at, :] = out.T.astype(BF16)
 
@@ -382,11 +377,11 @@
 
     own_ref[1] = jnp.zeros((8, 128), F32)
 
-    @pl.loop(0, TOK // 256)
+    @pl.loop(0, TOK // WIDE)
     def _(m):
-        at = pl.ds(pl.multiple_of(m * 256, 256), 256)
+        at = pl.ds(pl.multiple_of(m * WIDE, WIDE), WIDE)
         branch = jnp.dot(w2_ref[...], hid_ref[:, at], preferred_element_type=F32)
-        gate = jnp.concatenate([gate_ref[...], gate_ref[...]], axis=1)
+        gate = widened(gate_ref)
         mixed = tok_ref[:, at] + gate * branch
         center = mixed - jnp.sum(mixed, axis=0, keepdims=True) * (1.0 / D)
         variance = jnp.sum(center * center, axis=0, keepdims=True) * (1.0 / D)
@@ -408,6 +403,9 @@
 
     square_ref[...] = jnp.zeros_like(square_ref)
     chosen = selected_ref[0, 0] == 1
+    l0[0] = jnp.where(chosen, own_ref[1], 0.0)
+    losses = [remote(l0.at[0], l0.at[1], l_send.at[0], l_recv.at[0], partner)]
+    losses[0].start()
 
     def swap(f):
         return remote(send_ref.at[f], r0.at[f], q_send.at[f], q_recv.at[f], partner)
@@ -433,12 +431,17 @@
     total = jnp.sum(square_ref[...], axis=1, keepdims=True)
     factor = 1.0 / (jnp.sqrt(total * (1.0 / (2 * D * FF))) + clip_offset)
     own_ref[0] = jnp.broadcast_to(factor, (8, 128))
-    own_ref[1] = jnp.where(chosen, own_ref[1], 0.0)
-    loss_0 = remote(own_ref.at[pl.ds(0, 2)], own_ref.at[pl.ds(2, 2)], l_send.at[0], l_recv.at[0], partner)
-    loss_0.start()
+    factors = remote(own_ref.at[0], own_ref.at[2], l_send.at[7], l_recv.at[7], partner)
+    factors.start()
+    losses[0].wait_recv()
+    l1[x] = l0[0] + l0[1]
+    for k in range(1, NX):
+        copy = remote(l1.at[x], l1.at[x], l_send.at[k], l_recv.at[k], {"fsdp_1": x_at(k)})
+        copy.start()
+        losses.append(copy)
     for f in range(NY):
         swap(f).wait_recv()
-    loss_0.wait_recv()
+    factors.wait_recv()
     mine = own_ref[0, 0:1, 0:1]
     other = own_ref[2, 0:1, 0:1]
 
@@ -451,48 +454,25 @@
         at = part(half, k, j)
         return keep_ref[at] * mine + r0[at].astype(F32) * other
 
+    offsets = (2, 1, 3, 0)
     firsts = {}
-    for k in (2, 1, 3, 0):
-        for h in range(2):
-            for j in range(4):
-                value = chip(h, k, j)
-                if k == 0:
-                    acc[h, j] = value
-                else:
-                    s1[h, k - 1, j] = value.astype(BF16)
-            if k > 0:
-                firsts[h, k] = remote(
-                    s1.at[h, k - 1],
-                    r1.at[h, k - 1],
-                    s1_send.at[h, k],
-                    s1_recv.at[h, k],
+    for group in range(2):
+        for k in (2, 1, 3):
+            for h in range(2):
+                for q in (2 * group, 2 * group + 1):
+                    value = chip(h, k, second_at(h, offsets[q]))
+                    s1[h, k - 1, q] = value.astype(BF16)
+                firsts[h, k, group] = remote(
+                    s1.at[h, k - 1, pl.ds(2 * group, 2)],
+                    r1.at[h, k - 1, pl.ds(2 * group, 2)],
+                    s1_send.at[h, 2 * k + group],
+                    s1_recv.at[h, 2 * k + group],
                     first_to(h, k),
                 )
-                firsts[h, k].start()
-    l1[x] = own_ref[1] + own_ref[3]
-    losses = [loss_0]
-    for k in range(1, NX):
-        copy = remote(l1.at[x], l1.at[x], l_send.at[k], l_recv.at[k], {"fsdp_1": x_at(k)})
-        copy.start()
-        losses.append(copy)
-    seconds = {}
+                firsts[h, k, group].start()
     for h in range(2):
-        for k in (1, 3, 2):
-            firsts[h, k].wait_recv()
-        for k in (2, 1, 3, 0):
-            j = second_at(h, k)
-            acc[h, j] = (acc[h, j] + r1[h, 0, j].astype(F32)) + (
-                r1[h, 1, j].astype(F32) + r1[h, 2, j].astype(F32)
-            )
-            if k > 0:
-                seconds[h, k] = remote(
-                    acc.at[h, j],
-                    r2.at[h, k - 1],
-                    s2_send.at[h, k],
-                    s2_recv.at[h, k],
-                    second_to(h, k),
-                )
-                seconds[h, k].start()
+        for q in range(4):
+            acc[h, q] = chip(h, 0, second_at(h, offsets[q]))
     for copy in losses[1:]:
         copy.wait_recv()
     l2[y] = (l1[0] + l1[1]) + (l1[2] + l1[3])
@@ -502,21 +482,44 @@
         )
         copy.start()
         losses.append(copy)
-    for h in range(2):
-        for k in (1, 3, 2):
-            seconds[h, k].wait_recv()
-        j = second_at(h, 0)
-        value = (acc[h, j] + r2[h, 0]) + (r2[h, 1] + r2[h, 2])
-        for i in range(HALF // 8):
-            for n in range(D // 128):
-                t = (h * (HALF // 8) + i) * (D // 128) + n
-                tiles[t // PIECE, t % PIECE] = value[8 * i : 8 * i + 8, 128 * n : 128 * n + 128]
+    seconds = {}
+    for group in range(2):
+        for h in range(2):
+            for k in (1, 3, 2):
+                firsts[h, k, group].wait_recv()
+            for q in (2 * group, 2 * group + 1):
+                k = offsets[q]
+                value = (acc[h, q] + r1[h, 0, q].astype(F32)) + (
+                    r1[h, 1, q].astype(F32) + r1[h, 2, q].astype(F32)
+                )
+                if k == 0:
+                    acc[h, q] = value
+                else:
+                    c2[h, k - 1] = value.astype(BF16)
+                    seconds[h, k] = remote(
+                        c2.at[h, k - 1],
+                        r2.at[h, k - 1],
+                        s2_send.at[h, k],
+                        s2_recv.at[h, k],
+                        second_to(h, k),
+                    )
+                    seconds[h, k].start()
     for copy in losses[4:]:
         copy.wait_recv()
     at = USED_TILES
     tiles[at // PIECE, at % PIECE] = (l2[0] + l2[1]) + (l2[2] + l2[3])
     for t in range(USED_TILES + 1, TILES):
         tiles[t // PIECE, t % PIECE] = jnp.zeros((8, 128), F32)
+    for h in range(2):
+        for k in (1, 3, 2):
+            seconds[h, k].wait_recv()
+        value = (acc[h, 3] + r2[h, 0].astype(F32)) + (
+            r2[h, 1].astype(F32) + r2[h, 2].astype(F32)
+        )
+        for i in range(HALF // 8):
+            for n in range(D // 128):
+                t = (h * (HALF // 8) + i) * (D // 128) + n
+                tiles[t // PIECE, t % PIECE] = value[8 * i : 8 * i + 8, 128 * n : 128 * n + 128]
 
     order = (4, 3, 5, 2, 6, 1, 7)
     thirds = []
@@ -561,7 +564,7 @@
     for group in (early, late, crossed, firsts, seconds, spreads):
         for copy in group.values():
             copy.wait_send()
-    for group in (messages, losses, thirds, crossings):
+    for group in (messages, losses, thirds, crossings, [factors]):
         for copy in group:
             copy.wait_send()
 
@@ -606,16 +609,26 @@
             jax.ShapeDtypeStruct(tile, F32),
             jax.ShapeDtypeStruct((2 * SIDE, 128), F32),
         ),
-        in_specs=[SMEM_SPEC] * 5
-        + [ANY_SPEC]
-        + [VMEM_SPEC] * 8
-        + [ANY_SPEC] * 2
-        + [VMEM_SPEC],
+        in_specs=[ANY_SPEC] * 17,
         out_specs=(VMEM_SPEC,) * 3,
         scratch_shapes=[
+            pltpu.SMEM((1, AUG), jnp.int32),
+            pltpu.SMEM((2, AUG), jnp.int32),
+            pltpu.SMEM((1, AUG), jnp.int32),
+            pltpu.SMEM((1, 1), jnp.int32),
+            pltpu.SMEM((2, TSTEPS), F32),
             vmem((TOK, FCH), BF16),
+            vmem((72, FCH), BF16),
+            vmem((SHARD, D), BF16),
+            vmem((SHARD, D), BF16),
+            vmem((SIDE, 128), F32),
+            vmem((SIDE * AUG, 128), F32),
+            vmem((16, D), BF16),
+            vmem((96, D), BF16),
+            vmem((1, 128), F32),
             vmem((256, D), BF16),
             vmem((D, 3 * D), BF16),
+            vmem((16, D), BF16),
             vmem((2,) + grid, BF16),
             vmem((NDP,) + tile, F32),
             vmem((NDP,) + tile, F32),
@@ -641,17 +654,20 @@
             vmem((2, 3, 4, HALF, D), BF16),
             vmem((2, 3, 4, HALF, D), BF16),
             vmem((2, 4, HALF, D), F32),
-            vmem((2, 3, HALF, D), F32),
+            vmem((2, 3, HALF, D), BF16),
+            vmem((2, 3, HALF, D), BF16),
             vmem((NZ, PIECE) + tile, F32),
             vmem((NZ, PIECE) + tile, F32),
             vmem((2, NZ, PIECE) + tile, F32),
+            vmem((2,) + tile, F32),
             vmem((NX,) + tile, F32),
             vmem((NY,) + tile, F32),
         ]
-        + [dma((2, 4))] * 10
+        + [dma((2, 4))] * 8
+        + [dma((2, 8))] * 2
         + [dma((NDP,))] * 2
         + [dma((NZ,))] * 10
-        + [dma((3,))],
+        + [dma((17,))],
         compiler_params=pltpu.CompilerParams(
             collective_id=0, has_side_effects=True, vmem_limit_bytes=56 << 20
         ),

time: 76 us -> 71.7 us (0.943)
  Pallas kernels: 74.5 us -> 70.3 us
    pallas_call x1, Pallas kernels: 72.7 us -> 68.4 us  [per_device(): pl.pallas_call(step_kernel, out_shape=(jax.ShapeDtypeStruct((2, SHARD, D)...]
where the time goes in v4:
time: 71.7 us; the launch traced here: 71.6 us
  Pallas kernels  70.3 us (98%)
  between operations  1.29 us (2%)
    pallas_call x1, Pallas kernels, per_device(): pl.pallas_call(step_kernel, out_shape=(jax.ShapeDtypeStruct((2, SHARD, D)...  68.4 us
    pallas_call x1, Pallas kernels, per_device(): pl.pallas_call(finish_kernel, out_shape=(jax.ShapeDtypeStruct((SHARD, D),...  1.85 us

profile of v4, /device:TPU:1, one launch (start us, length us, event | category | flops | bytes accessed | tf_op | source)
XLA Modules:
  0.0 71.6 jit_solution(1181778146645801923)
XLA Ops:
  1.3 68.4 %step.1 = (f32[2,96,384]{2,1,0:T(8,128)}, f32[8,128]{1,0:T(8,128)}, f32[64,128]{1,0:T(8,128)}) custom-call(s32[1,4]{1,0:T(1,128)} %bitcast.34, s32[2,4]{1,0:T(2,128)} %bitcast.33, s32[1,4]{1,0:T(1,128)} %bitcast.35, s32[1,1]{1,0:T(1,128)S(6)} %copy.24.refs_3_, f32[2,1000]{1,0:T(2,128)} %constant.6.clone.refs_4_, bf16[1024,512]{1,0:T(8,128)(2,1)} %bitcast.24, ...), custom_call_target="tpu_custom_call" | custom-call | tf_op jit(solution)/shard_map/step/pallas_call | solution.py:605
  69.7 1.9 %finish.1 = (f32[96,384]{1,0:T(8,128)}, f32[96,384]{1,0:T(8,128)}, f32[1,1]{1,0:T(1,128)}, f32[64,128]{1,0:T(8,128)}) custom-call(f32[2,96,384]{2,1,0:T(8,128)} %get-tuple-element.11.sum_ref, f32[8,128]{1,0:T(8,128)} %get-tuple-element.12.total_ref, f32[64,128]{1,0:T(8,128)} %get-tuple-element.13.moved_ref, f32[96,384]{1,0:T(8,128)} %bitcast.25, ...), custom_call_target="tpu_custom_call" | custom-call | tf_op jit(solution)/shard_map/finish/pallas_call | solution.py:694

commit v5 on v4

--- a/solution.py
+++ b/solution.py
@@ -21,7 +21,7 @@
 SIDE, LC, AUG, TSTEPS = 32, 4, 4, 1000
 SELECTED = 128
 CHUNK = 384
-WIDE = 512
+WIDE = 1024
 PIECE = 5
 TILES = NZ * PIECE
 USED_TILES = (SHARD // 8) * (D // 128)
@@ -29,7 +29,7 @@
 noise_weight = 16.0
 norm_epsilon = 1e-06
 VMEM_SPEC = pl.BlockSpec(memory_space=pltpu.VMEM)
-ANY_SPEC = pl.BlockSpec(memory_space=pl.ANY)
+HBM_SPEC = pl.BlockSpec(memory_space=pltpu.HBM)
 SMEM_SPEC = pl.BlockSpec(memory_space=pltpu.SMEM)
 F32, BF16 = jnp.float32, jnp.bfloat16
 
@@ -98,8 +98,8 @@
     (square_ref, own_ref, keep_ref, send_ref, r0, s1, r1, acc, c2, r2) = scratch[17:27]
     (tiles, r3, whole, l0, l1, l2) = scratch[27:33]
     (g1_send, g1_recv, g2_send, g2_recv, p_send, p_recv) = scratch[33:39]
-    (s2_send, s2_recv, s1_send, s1_recv) = scratch[39:43]
-    (m_send, m_recv, q_send, q_recv, z_send, z_recv) = scratch[43:49]
+    (s2_send, s2_recv, q_send, q_recv, s1_send, s1_recv) = scratch[39:45]
+    (m_send, m_recv, z_send, z_recv) = scratch[45:49]
     (a_send, a_recv, f_send, f_recv, l_send, l_recv, c_sem) = scratch[49:]
     z, c, y, x = place()
     me = z * NC + c
@@ -328,11 +328,6 @@
         preferred_element_type=F32,
     )
 
-    for k in (1, 3):
-        for h in range(2):
-            late[h, k].wait_recv()
-            crossed[h, k].start()
-
     @pl.loop(0, TOK // WIDE)
     def _(m):
         at = pl.ds(pl.multiple_of(m * WIDE, WIDE), WIDE)
@@ -344,29 +339,18 @@
         modt_ref[:, at] = out.astype(BF16)
         mod_ref[at, :] = out.T.astype(BF16)
 
-    for k in (2,):
+    def weights(w, k):
+        near = all_ref[w, y_at(NY - k), :, 0].reshape(CHUNK // 2, D)
+        other = all_ref[w, :, x_at(NX - k), 1].reshape(CHUNK // 2, D)
+        return jnp.concatenate([near, other], axis=0)
+
+    root = math.sqrt(2.0 / math.pi)
+
+    def forward(k):
         for h in range(2):
-            late[h, k].wait_recv()
-            crossed[h, k].start()
-
-    for copy in crossed.values():
-        copy.wait_recv()
-    flat_weights = all_ref.reshape(2, FF, D)
-
-    def weights(w, at):
-        return flat_weights[w, at, :]
-
-    @pl.loop(0, FF // 128)
-    def _(m):
-        at = pl.ds(pl.multiple_of(m * 128, 128), 128)
-        w2_ref[:, at] = weights(1, at).astype(F32).T.astype(BF16)
-
-    root = math.sqrt(2.0 / math.pi)
-
-    @pl.loop(0, FF // CHUNK)
-    def _(f):
-        at = pl.ds(pl.multiple_of(f * CHUNK, CHUNK), CHUNK)
-        pre = jnp.dot(weights(0, at), modt_ref[...], preferred_element_type=F32)
+            crossed[h, k].wait_recv()
+        at = pl.ds(k * CHUNK, CHUNK)
+        pre = jnp.dot(weights(0, k), modt_ref[...], preferred_element_type=F32)
         squared = pre * pre
         inner = pre * (squared * (root * 0.044715) + root)
         share = 0.5 * jnp.tanh(inner) + 0.5
@@ -374,6 +358,20 @@
         hid_ref[at, :] = hidden.astype(BF16)
         slope = (1.0 - share) * hidden * (squared * (6.0 * root * 0.044715) + 2.0 * root)
         slope_ref[at, :] = slope + share
+        w2_ref[:, at] = weights(1, k).astype(F32).T.astype(BF16)
+
+    def pass_on(k):
+        for h in range(2):
+            late[h, k].wait_recv()
+            crossed[h, k].start()
+
+    forward(0)
+    pass_on(1)
+    pass_on(3)
+    forward(1)
+    pass_on(2)
+    forward(3)
+    forward(2)
 
     own_ref[1] = jnp.zeros((8, 128), F32)
 
@@ -407,23 +405,36 @@
     losses = [remote(l0.at[0], l0.at[1], l_send.at[0], l_recv.at[0], partner)]
     losses[0].start()
 
-    def swap(f):
-        return remote(send_ref.at[f], r0.at[f], q_send.at[f], q_recv.at[f], partner)
-
-    @pl.loop(0, NY)
-    def _(f):
-        at = pl.ds(pl.multiple_of(f * CHUNK, CHUNK), CHUNK)
-        grad_hidden = jnp.dot(weights(1, at), gbt_ref[...], preferred_element_type=F32)
+    def swap(half, k):
+        if half == 0:
+            at = (y_at(NY - k), slice(None), 0)
+        else:
+            at = (slice(None), x_at(NX - k), 1)
+        return remote(
+            send_ref.at[at], r0.at[at], q_send.at[half, k], q_recv.at[half, k], partner
+        )
+
+    for k in range(4):
+        at = pl.ds(k * CHUNK, CHUNK)
+        grad_hidden = jnp.dot(weights(1, k), gbt_ref[...], preferred_element_type=F32)
         grad_pre = (slope_ref[at, :] * grad_hidden).astype(BF16)
         grad_1 = jnp.dot(grad_pre, mod_ref[...], preferred_element_type=F32)
         grad_2 = jnp.dot(hid_ref[at, :], gb_ref[...], preferred_element_type=F32)
         grad_1 = jnp.where(chosen, grad_1, 0.0)
         grad_2 = jnp.where(chosen, grad_2, 0.0)
         kept = jnp.where(c == 0, grad_1, grad_2)
-        sent = jnp.where(c == 0, grad_2, grad_1)
-        keep_ref[f] = kept.reshape(NX, 2, HALF, D)
-        send_ref[f] = sent.astype(BF16).reshape(NX, 2, HALF, D)
-        swap(f).start()
+        sent = jnp.where(c == 0, grad_2, grad_1).astype(BF16)
+        for h in range(2):
+            rows = slice(h * CHUNK // 2, (h + 1) * CHUNK // 2)
+            kept_half = kept[rows].reshape(4, HALF, D)
+            sent_half = sent[rows].reshape(4, HALF, D)
+            if h == 0:
+                keep_ref[y_at(NY - k), :, 0] = kept_half
+                send_ref[y_at(NY - k), :, 0] = sent_half
+            else:
+                keep_ref[:, x_at(NX - k), 1] = kept_half
+                send_ref[:, x_at(NX - k), 1] = sent_half
+            swap(h, k).start()
         square_ref[...] += jnp.sum(
             grad_1 * grad_1 + grad_2 * grad_2, axis=0, keepdims=True
         )
@@ -439,8 +450,9 @@
         copy = remote(l1.at[x], l1.at[x], l_send.at[k], l_recv.at[k], {"fsdp_1": x_at(k)})
         copy.start()
         losses.append(copy)
-    for f in range(NY):
-        swap(f).wait_recv()
+    for k in range(4):
+        for h in range(2):
+            swap(h, k).wait_recv()
     factors.wait_recv()
     mine = own_ref[0, 0:1, 0:1]
     other = own_ref[2, 0:1, 0:1]
@@ -559,8 +571,9 @@
                 w, t // PIECE, t % PIECE
             ]
     total_ref[...] = whole[0, USED_TILES // PIECE, USED_TILES % PIECE]
-    for f in range(NY):
-        swap(f).wait_send()
+    for k in range(4):
+        for h in range(2):
+            swap(h, k).wait_send()
     for group in (early, late, crossed, firsts, seconds, spreads):
         for copy in group.values():
             copy.wait_send()
@@ -609,7 +622,7 @@
             jax.ShapeDtypeStruct(tile, F32),
             jax.ShapeDtypeStruct((2 * SIDE, 128), F32),
         ),
-        in_specs=[ANY_SPEC] * 17,
+        in_specs=[HBM_SPEC] * 17,
         out_specs=(VMEM_SPEC,) * 3,
         scratch_shapes=[
             pltpu.SMEM((1, AUG), jnp.int32),
@@ -663,10 +676,10 @@
             vmem((NX,) + tile, F32),
             vmem((NY,) + tile, F32),
         ]
-        + [dma((2, 4))] * 8
+        + [dma((2, 4))] * 10
         + [dma((2, 8))] * 2
         + [dma((NDP,))] * 2
-        + [dma((NZ,))] * 10
+        + [dma((NZ,))] * 8
         + [dma((17,))],
         compiler_params=pltpu.CompilerParams(
             collective_id=0, has_side_effects=True, vmem_limit_bytes=56 << 20

time: 71.7 us -> 65.7 us (0.916)
  Pallas kernels: 70.3 us -> 64.3 us
    pallas_call x1, Pallas kernels: 68.4 us -> 62.4 us  [per_device(): pl.pallas_call(step_kernel, out_shape=(jax.ShapeDtypeStruct((2, SHARD, D)...]
where the time goes in v5:
time: 65.7 us; the launch traced here: 65.6 us
  Pallas kernels  64.3 us (98%)
  between operations  1.29 us (2%)
    pallas_call x1, Pallas kernels, per_device(): pl.pallas_call(step_kernel, out_shape=(jax.ShapeDtypeStruct((2, SHARD, D)...  62.4 us
    pallas_call x1, Pallas kernels, per_device(): pl.pallas_call(finish_kernel, out_shape=(jax.ShapeDtypeStruct((SHARD, D),...  1.85 us

profile of v5, /device:TPU:1, one launch (start us, length us, event | category | flops | bytes accessed | tf_op | source)
XLA Modules:
  0.0 65.6 jit_solution(2653737621752143583)
XLA Ops:
  1.3 62.4 %step.1 = (f32[2,96,384]{2,1,0:T(8,128)}, f32[8,128]{1,0:T(8,128)}, f32[64,128]{1,0:T(8,128)}) custom-call(s32[1,4]{1,0:T(1,128)} %bitcast.34, s32[2,4]{1,0:T(2,128)} %bitcast.33, s32[1,4]{1,0:T(1,128)} %bitcast.35, s32[1,1]{1,0:T(1,128)S(6)} %copy.24.refs_3_, f32[2,1000]{1,0:T(2,128)} %constant.6.clone.refs_4_, bf16[1024,512]{1,0:T(8,128)(2,1)} %bitcast.24, ...), custom_call_target="tpu_custom_call" | custom-call | tf_op jit(solution)/shard_map/step/pallas_call | solution.py:618
  63.7 1.9 %finish.1 = (f32[96,384]{1,0:T(8,128)}, f32[96,384]{1,0:T(8,128)}, f32[1,1]{1,0:T(1,128)}, f32[64,128]{1,0:T(8,128)}) custom-call(f32[2,96,384]{2,1,0:T(8,128)} %get-tuple-element.11.sum_ref, f32[8,128]{1,0:T(8,128)} %get-tuple-element.12.total_ref, f32[64,128]{1,0:T(8,128)} %get-tuple-element.13.moved_ref, f32[96,384]{1,0:T(8,128)} %bitcast.25, ...), custom_call_target="tpu_custom_call" | custom-call | tf_op jit(solution)/shard_map/finish/pallas_call | solution.py:707

commit v6 on v5

--- a/solution.py
+++ b/solution.py
@@ -22,9 +22,7 @@
 SELECTED = 128
 CHUNK = 384
 WIDE = 1024
-PIECE = 5
-TILES = NZ * PIECE
-USED_TILES = (SHARD // 8) * (D // 128)
+BATCHES, ROWS = 3, 16
 clip_offset = 1e-05
 noise_weight = 16.0
 norm_epsilon = 1e-06
@@ -96,11 +94,11 @@
     (rows_ref, pads_ref, shift_ref, scale_ref, gate_ref, tok_ref, modt_ref) = scratch[3:10]
     (mod_ref, w2_ref, hid_ref, slope_ref, target_ref, gbt_ref, gb_ref) = scratch[10:17]
     (square_ref, own_ref, keep_ref, send_ref, r0, s1, r1, acc, c2, r2) = scratch[17:27]
-    (tiles, r3, whole, l0, l1, l2) = scratch[27:33]
-    (g1_send, g1_recv, g2_send, g2_recv, p_send, p_recv) = scratch[33:39]
-    (s2_send, s2_recv, q_send, q_recv, s1_send, s1_recv) = scratch[39:45]
-    (m_send, m_recv, z_send, z_recv) = scratch[45:49]
-    (a_send, a_recv, f_send, f_recv, l_send, l_recv, c_sem) = scratch[49:]
+    (tiles, r3, whole, l0, l1, l2, l3) = scratch[27:34]
+    (g1_send, g1_recv, g2_send, g2_recv, p_send, p_recv) = scratch[34:40]
+    (q_send, q_recv, s1_send, s1_recv, s2_send, s2_recv) = scratch[40:46]
+    (z_send, z_recv, a_send, a_recv) = scratch[46:50]
+    (m_send, m_recv, l_send, l_recv, f_send, f_recv, c_sem) = scratch[50:]
     z, c, y, x = place()
     me = z * NC + c
     partner = {"dp_1": 1 - c}
@@ -457,34 +455,31 @@
     mine = own_ref[0, 0:1, 0:1]
     other = own_ref[2, 0:1, 0:1]
 
-    def part(half, k, j):
-        if half == 0:
-            return (j, x_at(k), 0)
-        return (y_at(k), j, 1)
-
-    def chip(half, k, j):
-        at = part(half, k, j)
+    def chip(half, k, j, b):
+        rows = pl.ds(b * ROWS, ROWS)
+        at = (j, x_at(k), 0, rows) if half == 0 else (y_at(k), j, 1, rows)
         return keep_ref[at] * mine + r0[at].astype(F32) * other
 
     offsets = (2, 1, 3, 0)
-    firsts = {}
-    for group in range(2):
+    firsts, seconds, thirds, spreads, crossings = {}, {}, {}, {}, {}
+    for b in range(BATCHES):
         for k in (2, 1, 3):
             for h in range(2):
-                for q in (2 * group, 2 * group + 1):
-                    value = chip(h, k, second_at(h, offsets[q]))
-                    s1[h, k - 1, q] = value.astype(BF16)
-                firsts[h, k, group] = remote(
-                    s1.at[h, k - 1, pl.ds(2 * group, 2)],
-                    r1.at[h, k - 1, pl.ds(2 * group, 2)],
-                    s1_send.at[h, 2 * k + group],
-                    s1_recv.at[h, 2 * k + group],
+                for q in range(4):
+                    value = chip(h, k, second_at(h, offsets[q]), b)
+                    s1[b, h, k - 1, q] = value.astype(BF16)
+                firsts[b, h, k] = remote(
+                    s1.at[b, h, k - 1],
+                    r1.at[b, h, k - 1],
+                    s1_send.at[b, h, k],
+                    s1_recv.at[b, h, k],
                     first_to(h, k),
                 )
-                firsts[h, k, group].start()
-    for h in range(2):
-        for q in range(4):
-            acc[h, q] = chip(h, 0, second_at(h, offsets[q]))
+                firsts[b, h, k].start()
+    for b in range(BATCHES):
+        for h in range(2):
+            for q in range(4):
+                acc[b, h, q] = chip(h, 0, second_at(h, offsets[q]), b)
     for copy in losses[1:]:
         copy.wait_recv()
     l2[y] = (l1[0] + l1[1]) + (l1[2] + l1[3])
@@ -494,90 +489,112 @@
         )
         copy.start()
         losses.append(copy)
-    seconds = {}
-    for group in range(2):
+
+    def add_first(b):
         for h in range(2):
             for k in (1, 3, 2):
-                firsts[h, k, group].wait_recv()
-            for q in (2 * group, 2 * group + 1):
+                firsts[b, h, k].wait_recv()
+            for q in range(4):
                 k = offsets[q]
-                value = (acc[h, q] + r1[h, 0, q].astype(F32)) + (
-                    r1[h, 1, q].astype(F32) + r1[h, 2, q].astype(F32)
+                value = (acc[b, h, q] + r1[b, h, 0, q].astype(F32)) + (
+                    r1[b, h, 1, q].astype(F32) + r1[b, h, 2, q].astype(F32)
                 )
                 if k == 0:
-                    acc[h, q] = value
+                    acc[b, h, q] = value
                 else:
-                    c2[h, k - 1] = value.astype(BF16)
-                    seconds[h, k] = remote(
-                        c2.at[h, k - 1],
-                        r2.at[h, k - 1],
-                        s2_send.at[h, k],
-                        s2_recv.at[h, k],
+                    c2[b, h, k - 1] = value.astype(BF16)
+                    seconds[b, h, k] = remote(
+                        c2.at[b, h, k - 1],
+                        r2.at[b, h, k - 1],
+                        s2_send.at[b, h, k],
+                        s2_recv.at[b, h, k],
                         second_to(h, k),
                     )
-                    seconds[h, k].start()
+                    seconds[b, h, k].start()
+
+    order = (4, 3, 5, 2, 6, 1, 7)
+
+    def add_second(b):
+        for h in range(2):
+            for k in (1, 3, 2):
+                seconds[b, h, k].wait_recv()
+            value = (acc[b, h, 3] + r2[b, h, 0].astype(F32)) + (
+                r2[b, h, 1].astype(F32) + r2[b, h, 2].astype(F32)
+            )
+            for i in range(4):
+                tiles[b, 4 * h + i] = value[4 * i : 4 * i + 4]
+        for k in order:
+            thirds[b, k] = remote(
+                tiles.at[b, z_at(k)],
+                r3.at[b, z],
+                z_send.at[b, k],
+                z_recv.at[b, k],
+                {"dp_0": z_at(k)},
+            )
+            thirds[b, k].start()
+        r3[b, z] = tiles[b, z]
+
+    def add_third(b):
+        for k in order:
+            thirds[b, k].wait_recv()
+        value = r3[b, 0]
+        for k in range(1, NZ):
+            value = value + r3[b, k]
+        whole[c, b, z] = value
+        for k in order:
+            at = whole.at[c, b, z]
+            spreads[b, k] = remote(
+                at, at, a_send.at[b, k], a_recv.at[b, k], {"dp_0": z_at(k)}
+            )
+            spreads[b, k].start()
+
+    def cross(b):
+        for k in order:
+            spreads[b, k].wait_recv()
+        at = whole.at[c, b]
+        crossings[b] = remote(at, at, f_send.at[b], f_recv.at[b], partner)
+        crossings[b].start()
+
+    add_first(0)
+    add_first(1)
+    add_second(0)
     for copy in losses[4:]:
         copy.wait_recv()
-    at = USED_TILES
-    tiles[at // PIECE, at % PIECE] = (l2[0] + l2[1]) + (l2[2] + l2[3])
-    for t in range(USED_TILES + 1, TILES):
-        tiles[t // PIECE, t % PIECE] = jnp.zeros((8, 128), F32)
-    for h in range(2):
-        for k in (1, 3, 2):
-            seconds[h, k].wait_recv()
-        value = (acc[h, 3] + r2[h, 0].astype(F32)) + (
-            r2[h, 1].astype(F32) + r2[h, 2].astype(F32)
-        )
-        for i in range(HALF // 8):
-            for n in range(D // 128):
-                t = (h * (HALF // 8) + i) * (D // 128) + n
-                tiles[t // PIECE, t % PIECE] = value[8 * i : 8 * i + 8, 128 * n : 128 * n + 128]
-
-    order = (4, 3, 5, 2, 6, 1, 7)
-    thirds = []
-    for k in order:
+    l3[z] = (l2[0] + l2[1]) + (l2[2] + l2[3])
+    for k in range(1, NZ):
         copy = remote(
-            tiles.at[z_at(k)], r3.at[z], z_send.at[k], z_recv.at[k], {"dp_0": z_at(k)}
+            l3.at[z], l3.at[z], l_send.at[7 + k], l_recv.at[7 + k], {"dp_0": z_at(k)}
         )
         copy.start()
-        thirds.append(copy)
-    r3[z] = tiles[z]
-    for copy in thirds:
+        losses.append(copy)
+    add_first(2)
+    add_second(1)
+    add_third(0)
+    add_second(2)
+    add_third(1)
+    cross(0)
+    add_third(2)
+    cross(1)
+    cross(2)
+    for copy in losses[7:]:
         copy.wait_recv()
-    value = r3[0]
+    value = l3[0]
     for k in range(1, NZ):
-        value = value + r3[k]
-    whole[c, z] = value
-    spreads = {}
-    for k in order:
-        spreads[k] = remote(
-            whole.at[c, z], whole.at[c, z], a_send.at[k], a_recv.at[k], {"dp_0": z_at(k)}
-        )
-        spreads[k].start()
-    crossings = []
-    for k in (0, 7, 1, 6, 2, 5, 3, 4):
-        if k > 0:
-            spreads[k].wait_recv()
-        at = z_at(NZ - k) if k > 0 else z
-        copy = remote(whole.at[c, at], whole.at[c, at], f_send.at[k], f_recv.at[k], partner)
-        copy.start()
-        crossings.append(copy)
-    for copy in crossings:
-        copy.wait_recv()
-    for w in range(2):
-        for t in range(USED_TILES):
-            i, n = t // (D // 128), t % (D // 128)
-            sum_ref[w, 8 * i : 8 * i + 8, 128 * n : 128 * n + 128] = whole[
-                w, t // PIECE, t % PIECE
-            ]
-    total_ref[...] = whole[0, USED_TILES // PIECE, USED_TILES % PIECE]
+        value = value + l3[k]
+    total_ref[...] = value
+    for b in range(BATCHES):
+        crossings[b].wait_recv()
+        for w in range(2):
+            for i in range(NZ):
+                at = (i // 4) * HALF + b * ROWS + (i % 4) * 4
+                sum_ref[w, at : at + 4, :] = whole[w, b, i]
     for k in range(4):
         for h in range(2):
             swap(h, k).wait_send()
-    for group in (early, late, crossed, firsts, seconds, spreads):
+    for group in (early, late, crossed, firsts, seconds, thirds, spreads, crossings):
         for copy in group.values():
             copy.wait_send()
-    for group in (messages, losses, thirds, crossings, [factors]):
+    for group in (messages, losses, [factors]):
         for copy in group:
             copy.wait_send()
 
@@ -664,22 +681,24 @@
             vmem(grid, F32),
             vmem(grid, BF16),
             vmem(grid, BF16),
-            vmem((2, 3, 4, HALF, D), BF16),
-            vmem((2, 3, 4, HALF, D), BF16),
-            vmem((2, 4, HALF, D), F32),
-            vmem((2, 3, HALF, D), BF16),
-            vmem((2, 3, HALF, D), BF16),
-            vmem((NZ, PIECE) + tile, F32),
-            vmem((NZ, PIECE) + tile, F32),
-            vmem((2, NZ, PIECE) + tile, F32),
+            vmem((BATCHES, 2, 3, 4, ROWS, D), BF16),
+            vmem((BATCHES, 2, 3, 4, ROWS, D), BF16),
+            vmem((BATCHES, 2, 4, ROWS, D), F32),
+            vmem((BATCHES, 2, 3, ROWS, D), BF16),
+            vmem((BATCHES, 2, 3, ROWS, D), BF16),
+            vmem((BATCHES, NZ, 4, D), F32),
+            vmem((BATCHES, NZ, 4, D), F32),
+            vmem((2, BATCHES, NZ, 4, D), F32),
             vmem((2,) + tile, F32),
             vmem((NX,) + tile, F32),
             vmem((NY,) + tile, F32),
+            vmem((NZ,) + tile, F32),
         ]
-        + [dma((2, 4))] * 10
-        + [dma((2, 8))] * 2
-        + [dma((NDP,))] * 2
-        + [dma((NZ,))] * 8
+        + [dma((2, 4))] * 8
+        + [dma((BATCHES, 2, 4))] * 4
+        + [dma((BATCHES, NZ))] * 4
+        + [dma((NDP,))] * 4
+        + [dma((BATCHES,))] * 2
         + [dma((17,))],
         compiler_params=pltpu.CompilerParams(
             collective_id=0, has_side_effects=True, vmem_limit_bytes=56 << 20

time: 65.7 us -> 69.3 us (1.055)
  Pallas kernels: 64.3 us -> 67.9 us
    pallas_call x1, Pallas kernels: 62.4 us -> 66 us  [per_device(): pl.pallas_call(step_kernel, out_shape=(jax.ShapeDtypeStruct((2, SHARD, D)...]
where the time goes in v6:
time: 69.3 us; the launch traced here: 69.2 us
  Pallas kernels  67.9 us (98%)
  between operations  1.29 us (2%)
    pallas_call x1, Pallas kernels, per_device(): pl.pallas_call(step_kernel, out_shape=(jax.ShapeDtypeStruct((2, SHARD, D)...  66 us
    pallas_call x1, Pallas kernels, per_device(): pl.pallas_call(finish_kernel, out_shape=(jax.ShapeDtypeStruct((SHARD, D),...  1.85 us

profile of v6, /device:TPU:1, one launch (start us, length us, event | category | flops | bytes accessed | tf_op | source)
XLA Modules:
  0.0 69.2 jit_solution(15334259285418287250)
XLA Ops:
  1.3 66.0 %step.1 = (f32[2,96,384]{2,1,0:T(8,128)}, f32[8,128]{1,0:T(8,128)}, f32[64,128]{1,0:T(8,128)}) custom-call(s32[1,4]{1,0:T(1,128)} %bitcast.34, s32[2,4]{1,0:T(2,128)} %bitcast.33, s32[1,4]{1,0:T(1,128)} %bitcast.35, s32[1,1]{1,0:T(1,128)S(6)} %copy.24.refs_3_, f32[2,1000]{1,0:T(2,128)} %constant.6.clone.refs_4_, bf16[1024,512]{1,0:T(8,128)(2,1)} %bitcast.24, ...), custom_call_target="tpu_custom_call" | custom-call | tf_op jit(solution)/shard_map/step/pallas_call | solution.py:635
  67.3 1.9 %finish.1 = (f32[96,384]{1,0:T(8,128)}, f32[96,384]{1,0:T(8,128)}, f32[1,1]{1,0:T(1,128)}, f32[64,128]{1,0:T(8,128)}) custom-call(f32[2,96,384]{2,1,0:T(8,128)} %get-tuple-element.11.sum_ref, f32[8,128]{1,0:T(8,128)} %get-tuple-element.12.total_ref, f32[64,128]{1,0:T(8,128)} %get-tuple-element.13.moved_ref, f32[96,384]{1,0:T(8,128)} %bitcast.25, ...), custom_call_target="tpu_custom_call" | custom-call | tf_op jit(solution)/shard_map/finish/pallas_call | solution.py:726

commit v7 on v5

--- a/solution.py
+++ b/solution.py
@@ -23,6 +23,7 @@
 CHUNK = 384
 WIDE = 1024
 PIECE = 5
+FAR = (3, 4, 5)
 TILES = NZ * PIECE
 USED_TILES = (SHARD // 8) * (D // 128)
 clip_offset = 1e-05
@@ -96,11 +97,11 @@
     (rows_ref, pads_ref, shift_ref, scale_ref, gate_ref, tok_ref, modt_ref) = scratch[3:10]
     (mod_ref, w2_ref, hid_ref, slope_ref, target_ref, gbt_ref, gb_ref) = scratch[10:17]
     (square_ref, own_ref, keep_ref, send_ref, r0, s1, r1, acc, c2, r2) = scratch[17:27]
-    (tiles, r3, whole, l0, l1, l2) = scratch[27:33]
-    (g1_send, g1_recv, g2_send, g2_recv, p_send, p_recv) = scratch[33:39]
-    (s2_send, s2_recv, q_send, q_recv, s1_send, s1_recv) = scratch[39:45]
-    (m_send, m_recv, z_send, z_recv) = scratch[45:49]
-    (a_send, a_recv, f_send, f_recv, l_send, l_recv, c_sem) = scratch[49:]
+    (tiles, r3, whole, l0, l1, l2, far_ref, r3_far) = scratch[27:35]
+    (g1_send, g1_recv, g2_send, g2_recv, p_send, p_recv) = scratch[35:41]
+    (s2_send, s2_recv, q_send, q_recv, s1_send, s1_recv) = scratch[41:47]
+    (m_send, m_recv, z_send, z_recv) = scratch[47:51]
+    (a_send, a_recv, f_send, f_recv, l_send, l_recv, c_sem) = scratch[51:]
     z, c, y, x = place()
     me = z * NC + c
     partner = {"dp_1": 1 - c}
@@ -518,9 +519,12 @@
                     seconds[h, k].start()
     for copy in losses[4:]:
         copy.wait_recv()
+    plane = (l2[0] + l2[1]) + (l2[2] + l2[3])
+    coarse = plane.astype(BF16).astype(F32)
     at = USED_TILES
-    tiles[at // PIECE, at % PIECE] = (l2[0] + l2[1]) + (l2[2] + l2[3])
-    for t in range(USED_TILES + 1, TILES):
+    tiles[at // PIECE, at % PIECE] = coarse
+    tiles[at // PIECE, at % PIECE + 1] = plane - coarse
+    for t in range(USED_TILES + 2, TILES):
         tiles[t // PIECE, t % PIECE] = jnp.zeros((8, 128), F32)
     for h in range(2):
         for k in (1, 3, 2):
@@ -536,17 +540,23 @@
     order = (4, 3, 5, 2, 6, 1, 7)
     thirds = []
     for k in order:
-        copy = remote(
-            tiles.at[z_at(k)], r3.at[z], z_send.at[k], z_recv.at[k], {"dp_0": z_at(k)}
-        )
+        if k in FAR:
+            slot = k - FAR[0]
+            far_ref[slot] = tiles[z_at(k)].reshape(PIECE * 8, 128).astype(BF16)
+            src, dst = far_ref.at[slot], r3_far.at[slot]
+        else:
+            src, dst = tiles.at[z_at(k)], r3.at[k]
+        copy = remote(src, dst, z_send.at[k], z_recv.at[k], {"dp_0": z_at(k)})
         copy.start()
         thirds.append(copy)
-    r3[z] = tiles[z]
     for copy in thirds:
         copy.wait_recv()
-    value = r3[0]
+    value = tiles[z]
     for k in range(1, NZ):
-        value = value + r3[k]
+        if k in FAR:
+            value = value + r3_far[k - FAR[0]].astype(F32).reshape(PIECE, 8, 128)
+        else:
+            value = value + r3[k]
     whole[c, z] = value
     spreads = {}
     for k in order:
@@ -570,7 +580,8 @@
             sum_ref[w, 8 * i : 8 * i + 8, 128 * n : 128 * n + 128] = whole[
                 w, t // PIECE, t % PIECE
             ]
-    total_ref[...] = whole[0, USED_TILES // PIECE, USED_TILES % PIECE]
+    at = USED_TILES
+    total_ref[...] = whole[0, at // PIECE, at % PIECE] + whole[0, at // PIECE, at % PIECE + 1]
     for k in range(4):
         for h in range(2):
             swap(h, k).wait_send()
@@ -675,6 +686,8 @@
             vmem((2,) + tile, F32),
             vmem((NX,) + tile, F32),
             vmem((NY,) + tile, F32),
+            vmem((3, PIECE * 8, 128), BF16),
+            vmem((3, PIECE * 8, 128), BF16),
         ]
         + [dma((2, 4))] * 10
         + [dma((2, 8))] * 2

time: 65.7 us -> 65 us (0.989)
  Pallas kernels: 64.3 us -> 63.6 us
    pallas_call x1, Pallas kernels: 62.4 us -> 61.7 us  [per_device(): pl.pallas_call(step_kernel, out_shape=(jax.ShapeDtypeStruct((2, SHARD, D)...]
where the time goes in v7:
time: 65 us; the launch traced here: 64.8 us
  Pallas kernels  63.6 us (98%)
  between operations  1.29 us (2%)
    pallas_call x1, Pallas kernels, per_device(): pl.pallas_call(step_kernel, out_shape=(jax.ShapeDtypeStruct((2, SHARD, D)...  61.7 us
    pallas_call x1, Pallas kernels, per_device(): pl.pallas_call(finish_kernel, out_shape=(jax.ShapeDtypeStruct((SHARD, D),...  1.85 us

profile of v7, /device:TPU:1, one launch (start us, length us, event | category | flops | bytes accessed | tf_op | source)
XLA Modules:
  0.0 64.8 jit_solution(1155078810699710192)
XLA Ops:
  1.3 61.7 %step.1 = (f32[2,96,384]{2,1,0:T(8,128)}, f32[8,128]{1,0:T(8,128)}, f32[64,128]{1,0:T(8,128)}) custom-call(s32[1,4]{1,0:T(1,128)} %bitcast.34, s32[2,4]{1,0:T(2,128)} %bitcast.33, s32[1,4]{1,0:T(1,128)} %bitcast.35, s32[1,1]{1,0:T(1,128)S(6)} %copy.24.refs_3_, f32[2,1000]{1,0:T(2,128)} %constant.6.clone.refs_4_, bf16[1024,512]{1,0:T(8,128)(2,1)} %bitcast.24, ...), custom_call_target="tpu_custom_call" | custom-call | tf_op jit(solution)/shard_map/step/pallas_call | solution.py:629
  63.0 1.9 %finish.1 = (f32[96,384]{1,0:T(8,128)}, f32[96,384]{1,0:T(8,128)}, f32[1,1]{1,0:T(1,128)}, f32[64,128]{1,0:T(8,128)}) custom-call(f32[2,96,384]{2,1,0:T(8,128)} %get-tuple-element.11.sum_ref, f32[8,128]{1,0:T(8,128)} %get-tuple-element.12.total_ref, f32[64,128]{1,0:T(8,128)} %get-tuple-element.13.moved_ref, f32[96,384]{1,0:T(8,128)} %bitcast.25, ...), custom_call_target="tpu_custom_call" | custom-call | tf_op jit(solution)/shard_map/finish/pallas_call | solution.py:720

commit v8 on v7

--- a/solution.py
+++ b/solution.py
@@ -24,6 +24,7 @@
 WIDE = 1024
 PIECE = 5
 FAR = (3, 4, 5)
+GROUPS = ((0, 3), (3, 4))
 TILES = NZ * PIECE
 USED_TILES = (SHARD // 8) * (D // 128)
 clip_offset = 1e-05
@@ -470,14 +471,15 @@
     offsets = (2, 1, 3, 0)
     firsts = {}
     for group in range(2):
+        span = slice(*GROUPS[group])
         for k in (2, 1, 3):
             for h in range(2):
-                for q in (2 * group, 2 * group + 1):
+                for q in range(*GROUPS[group]):
                     value = chip(h, k, second_at(h, offsets[q]))
                     s1[h, k - 1, q] = value.astype(BF16)
                 firsts[h, k, group] = remote(
-                    s1.at[h, k - 1, pl.ds(2 * group, 2)],
-                    r1.at[h, k - 1, pl.ds(2 * group, 2)],
+                    s1.at[h, k - 1, span],
+                    r1.at[h, k - 1, span],
                     s1_send.at[h, 2 * k + group],
                     s1_recv.at[h, 2 * k + group],
                     first_to(h, k),
@@ -500,7 +502,7 @@
         for h in range(2):
             for k in (1, 3, 2):
                 firsts[h, k, group].wait_recv()
-            for q in (2 * group, 2 * group + 1):
+            for q in range(*GROUPS[group]):
                 k = offsets[q]
                 value = (acc[h, q] + r1[h, 0, q].astype(F32)) + (
                     r1[h, 1, q].astype(F32) + r1[h, 2, q].astype(F32)

time: 65 us -> 65.1 us (level)
  no operation moved by 1% of the time
where the time goes in v8:
time: 65.1 us; the launch traced here: 65 us
  Pallas kernels  63.7 us (98%)
  between operations  1.29 us (2%)
    pallas_call x1, Pallas kernels, per_device(): pl.pallas_call(step_kernel, out_shape=(jax.ShapeDtypeStruct((2, SHARD, D)...  61.9 us
    pallas_call x1, Pallas kernels, per_device(): pl.pallas_call(finish_kernel, out_shape=(jax.ShapeDtypeStruct((SHARD, D),...  1.85 us

profile of v8, /device:TPU:1, one launch (start us, length us, event | category | flops | bytes accessed | tf_op | source)
XLA Modules:
  0.0 65.0 jit_solution(13386836200877748814)
XLA Ops:
  1.3 61.9 %step.1 = (f32[2,96,384]{2,1,0:T(8,128)}, f32[8,128]{1,0:T(8,128)}, f32[64,128]{1,0:T(8,128)}) custom-call(s32[1,4]{1,0:T(1,128)} %bitcast.34, s32[2,4]{1,0:T(2,128)} %bitcast.33, s32[1,4]{1,0:T(1,128)} %bitcast.35, s32[1,1]{1,0:T(1,128)S(6)} %copy.24.refs_3_, f32[2,1000]{1,0:T(2,128)} %constant.6.clone.refs_4_, bf16[1024,512]{1,0:T(8,128)(2,1)} %bitcast.24, ...), custom_call_target="tpu_custom_call" | custom-call | tf_op jit(solution)/shard_map/step/pallas_call | solution.py:631
  63.2 1.9 %finish.1 = (f32[96,384]{1,0:T(8,128)}, f32[96,384]{1,0:T(8,128)}, f32[1,1]{1,0:T(1,128)}, f32[64,128]{1,0:T(8,128)}) custom-call(f32[2,96,384]{2,1,0:T(8,128)} %get-tuple-element.11.sum_ref, f32[8,128]{1,0:T(8,128)} %get-tuple-element.12.total_ref, f32[64,128]{1,0:T(8,128)} %get-tuple-element.13.moved_ref, f32[96,384]{1,0:T(8,128)} %bitcast.25, ...), custom_call_target="tpu_custom_call" | custom-call | tf_op jit(solution)/shard_map/finish/pallas_call | solution.py:722
